TPU v7x, 512 devices: a whole 4x8x8 slice. The times are simulated.
512 devices in a mesh: grp: 2 (over core), gx: 16 (over x_hi, y), gy: 16 (over x_lo, z).
Axes of the slice: x: 4 (x_hi: 2, x_lo: 2; x = x_hi * 2 + x_lo), y: 8, z: 8, core: 2. Of those that a mesh axis runs over, the one named last changes fastest.
Arguments:
- state_now: float32 [2, 128, 256, 256], P('grp', 'gx', 'gy'), may hold values from -6 to 6
- state_later: float32 [2, 128, 256, 256], P('grp', 'gx', 'gy'), may hold values from -6 to 6
- courant: float32 [128, 256, 256], P('gx', 'gy'), may hold values from 0.04 to 0.18
- strips: float32 [8, 128, 2048], P(None, 'gx', 'gy'), may hold values from -6 to 6
- traces: float32 [8, 16, 16, 128], P(None, 'gx', 'gy'), may hold values from -60 to 60
- receiver_cells: int32 [16, 16, 128], P('gx', 'gy'), may hold values from 0 to 32767
- source_point: int32 [3], replicated, may hold values from 0 to 127
- wavelet: float32 [8], replicated, may hold values from -100 to 100
Outputs:
- image_sum: float32 [128, 256, 256], P('gx', 'gy', 'grp')
- wave_now: float32 [2, 128, 256, 256], P('grp', 'gx', 'gy')
- wave_later: float32 [2, 128, 256, 256], P('grp', 'gx', 'gy')
Inputs may be any that keep to these rules, and one draw needn't show every extreme that they name: `receiver_cells`: index of the cell in its block, depth fastest, then crossline, then inline; several receivers may share a cell.
All inputs are finite; a program needn't handle non-finite values.
Results may differ from a plain program's by a relative error of at most 0.00002.
Values sent between devices are 32-bit elements; how exact they have to be, the bound alone decides.
A program may use at most 64 MiB of HBM per device.

v0:
```python
import jax
import jax.numpy as jnp
from jax import lax
from jax.sharding import PartitionSpec as P

STEPS = 8


STENCIL = (-205.0 / 72.0, 8.0 / 5.0, -1.0 / 5.0, 8.0 / 315.0, -1.0 / 560.0)


def from_partner(shard, axis, bit):
    return lax.ppermute(shard, axis, [(i, i ^ 1 << bit) for i in range(lax.axis_size(axis))])


def extended(shard, sides, width):
    edges = {}
    for axis, dim in sides:
        size, length = (lax.axis_size(axis), shard.shape[dim])
        up = [(i, (i + 1) % size) for i in range(size - 1)]
        last = lax.slice_in_dim(shard, length - width, length, axis=dim)
        initial = lax.slice_in_dim(shard, 0, width, axis=dim)
        edges[dim] = (
            lax.ppermute(last, axis, up),
            lax.ppermute(initial, axis, [(b, a) for a, b in up]),
        )
    done = []
    for _, dim in sides:
        low, high = edges[dim]
        around = [(width, width) if d in done else (0, 0) for d in range(shard.ndim)]
        shard = jnp.concatenate([jnp.pad(low, around), shard, jnp.pad(high, around)], axis=dim)
        done.append(dim)
    return shard


def laplacian(padded):
    span_x = padded.shape[-3] - 8
    span_y = padded.shape[-2] - 8
    span_z = padded.shape[-1] - 8

    def window(offset_x, offset_y, offset_z):
        return padded[
            ...,
            4 + offset_x : 4 + offset_x + span_x,
            4 + offset_y : 4 + offset_y + span_y,
            4 + offset_z : 4 + offset_z + span_z,
        ]

    accumulated = 3.0 * STENCIL[0] * window(0, 0, 0)
    for radius in range(1, 5):
        beside_all = (
            window(radius, 0, 0)
            + window(-radius, 0, 0)
            + window(0, radius, 0)
            + window(0, -radius, 0)
            + window(0, 0, radius)
            + window(0, 0, -radius)
        )
        accumulated = accumulated + STENCIL[radius] * beside_all
    return accumulated


def depth_pad(field):
    return jnp.pad(field, ((0, 0), (0, 0), (4, 4)))


def split_laplacian(local_field, padded):
    cells_x = local_field.shape[0]
    cells_y = local_field.shape[1]
    whole_pad = depth_pad(padded)
    interior = laplacian(depth_pad(local_field))
    x_lower = laplacian(whole_pad[0:12])
    x_upper = laplacian(whole_pad[cells_x - 4 : cells_x + 8])
    y_lower = laplacian(whole_pad[4 : cells_x + 4, 0:12])
    y_upper = laplacian(whole_pad[4 : cells_x + 4, cells_y - 4 : cells_y + 8])
    middle = jnp.concatenate([y_lower, interior, y_upper], axis=1)
    return jnp.concatenate([x_lower, middle, x_upper], axis=0)


def imaging(image_sum, newest, source_side):
    half_depth = newest.shape[2] // 2
    lower_half = newest[..., :half_depth]
    upper_half = newest[..., half_depth:]
    kept_half = jnp.where(source_side, lower_half, upper_half)
    sent_half = jnp.where(source_side, upper_half, lower_half)
    partner = from_partner(sent_half, "grp", 0)
    return image_sum + kept_half * partner


def local(state_now, state_later, courant, strips, traces, receiver_cells, source_point, wavelet):
    current = state_now[0]
    future = state_later[0]
    cells_x, cells_y, cells_z = current.shape
    total_cells = cells_x * cells_y * cells_z
    source_side = lax.axis_index("grp") == 0
    tile_x = lax.axis_index("gx")
    tile_y = lax.axis_index("gy")
    depth_idx = jnp.arange(cells_z, dtype=jnp.int32)
    strip_layer = ((depth_idx < 4) | (depth_idx >= cells_z - 4))[None, None, :]
    overwrite = jnp.logical_and(strip_layer, source_side)
    courant_flat = courant.reshape(-1)
    flat_cells = receiver_cells.reshape(-1)
    receiver_coef = courant_flat[flat_cells]
    source_x = source_point[0] - tile_x * cells_x
    source_y = source_point[1] - tile_y * cells_y
    inside = (source_x >= 0) & (source_x < cells_x) & (source_y >= 0) & (source_y < cells_y)
    source_flat = jnp.where(inside, (source_x * cells_y + source_y) * cells_z + source_point[2], 0)
    source_coef = jnp.where(inside, courant_flat[source_flat], 0.0)
    strip_cells = strips.reshape(strips.shape[0], cells_x, cells_y, 8)
    filler = jnp.zeros((cells_x, cells_y, cells_z - 8), jnp.float32)
    image_sum = jnp.zeros((cells_x, cells_y, cells_z // 2), jnp.float32)
    for moment in range(STEPS):
        padded = extended(current, (("gx", 0), ("gy", 1)), 4)
        curvature = split_laplacian(current, padded)
        computed = 2.0 * current - future + courant * curvature
        receiver_add = (
            jnp.zeros((total_cells,), jnp.float32)
            .at[flat_cells]
            .add(receiver_coef * traces[moment].reshape(-1))
            .reshape(cells_x, cells_y, cells_z)
        )
        source_add = (
            jnp.zeros((total_cells,), jnp.float32)
            .at[source_flat]
            .add(-source_coef * wavelet[moment])
            .reshape(cells_x, cells_y, cells_z)
        )
        strip_dense = jnp.concatenate(
            [strip_cells[moment][..., :4], filler, strip_cells[moment][..., 4:]], axis=-1
        )
        forcing_now = jnp.where(
            source_side, jnp.where(strip_layer, strip_dense, source_add), receiver_add
        )
        newest = jnp.where(overwrite, forcing_now, computed + forcing_now)
        future = current
        current = newest
        if (moment + 1) % 4 == 0:
            image_sum = imaging(image_sum, newest, source_side)
    return (image_sum, current[None], future[None])


def solution(mesh):
    in_specs = (
        P("grp", "gx", "gy", None),
        P("grp", "gx", "gy", None),
        P("gx", "gy", None),
        P(None, "gx", "gy"),
        P(None, "gx", "gy", None),
        P("gx", "gy", None),
        P(),
        P(),
    )
    out_specs = (P("gx", "gy", "grp"), P("grp", "gx", "gy", None), P("grp", "gx", "gy", None))
    return jax.shard_map(local, mesh=mesh, in_specs=in_specs, out_specs=out_specs, check_vma=False)
```

profile of v0, /device:TPU:7, one launch (start us, length us, event | category | flops | bytes accessed | tf_op | source)
XLA Modules:
  0.0 190.8 jit_solution(14213848954922337598)
XLA Ops:
  1.6 10.9 %collective-permute-start.2 = (f32[8,4,256]{2,1,0:T(4,128)S(1)}, f32[8,4,256]{2,1,0:T(4,128)S(1)}, u32[]{:S(2)}, u32[]{:S(2)}) collective-permute-start(f32[8,4,256]{2,1,0:T(4,128)S(1)} %get-tuple-element.146), channel_id=1, source_target_pairs={{1,0},{2,1},{3,2},{4,3},{5,4},{6,5},{7,6},{8,7},{9,8},{10,9},{11,1... | collective-permute-start | bytes 98312 | tf_op jit(solution)/shard_map/ppermute | solution.py:25
  12.5 2.1 %collective-permute-start.3 = (f32[8,4,256]{2,1,0:T(4,128)S(1)}, f32[8,4,256]{2,1,0:T(4,128)S(1)}, u32[]{:S(2)}, u32[]{:S(2)}) collective-permute-start(f32[8,4,256]{2,1,0:T(4,128)S(1)} %get-tuple-element.145), channel_id=1, source_target_pairs={{0,1},{1,2},{2,3},{3,4},{4,5},{5,6},{6,7},{7,8},{8,9},{9,10},{10,1... | collective-permute-start | bytes 98312 | tf_op jit(solution)/shard_map/ppermute | solution.py:24
  14.6 3.2 %collective-permute-start = (f32[4,16,256]{2,1,0:T(8,128)S(1)}, f32[4,16,256]{2,1,0:T(8,128)S(1)}, u32[]{:S(2)}, u32[]{:S(2)}) collective-permute-start(f32[4,16,256]{2,1,0:T(8,128)S(1)} %get-tuple-element.143), channel_id=1, source_target_pairs={{0,16},{16,32},{32,48},{48,64},{64,80},{80,96},{96,112},{112,128},... | collective-permute-start | bytes 196616 | tf_op jit(solution)/shard_map/ppermute | solution.py:24
  17.8 5.7 %collective-permute-start.1 = (f32[4,16,256]{2,1,0:T(8,128)S(1)}, f32[4,16,256]{2,1,0:T(8,128)S(1)}, u32[]{:S(2)}, u32[]{:S(2)}) collective-permute-start(f32[4,16,256]{2,1,0:T(8,128)S(1)} %get-tuple-element.144), channel_id=1, source_target_pairs={{16,0},{32,16},{48,32},{64,48},{80,64},{96,80},{112,96},{128,112},... | collective-permute-start | bytes 196616 | tf_op jit(solution)/shard_map/ppermute | solution.py:25
  36.3 7.0 %collective-permute-start.5 = (f32[4,16,256]{2,1,0:T(8,128)S(1)}, f32[4,16,256]{2,1,0:T(8,128)S(1)}, u32[]{:S(2)}, u32[]{:S(2)}) collective-permute-start(f32[4,16,256]{2,1,0:T(8,128)S(1)} %get-tuple-element.140), channel_id=1, source_target_pairs={{16,0},{32,16},{48,32},{64,48},{80,64},{96,80},{112,96},{128,112},... | collective-permute-start | bytes 196616 | tf_op jit(solution)/shard_map/ppermute | solution.py:25
  43.3 5.5 %collective-permute-start.6 = (f32[8,4,256]{2,1,0:T(4,128)S(1)}, f32[8,4,256]{2,1,0:T(4,128)S(1)}, u32[]{:S(2)}, u32[]{:S(2)}) collective-permute-start(f32[8,4,256]{2,1,0:T(4,128)S(1)} %get-tuple-element.142), channel_id=1, source_target_pairs={{1,0},{2,1},{3,2},{4,3},{5,4},{6,5},{7,6},{8,7},{9,8},{10,9},{11,1... | collective-permute-start | bytes 98312 | tf_op jit(solution)/shard_map/ppermute | solution.py:25
  53.0 2.5 %collective-permute-done.7 = f32[8,4,256]{2,1,0:T(4,128)S(1)} collective-permute-done((f32[8,4,256]{2,1,0:T(4,128)S(1)}, f32[8,4,256]{2,1,0:T(4,128)S(1)}, u32[]{:S(2)}, u32[]{:S(2)}) %collective-permute-start.7) | collective-permute-done | bytes 32800 | tf_op jit(solution)/shard_map/ppermute | solution.py:24
  58.4 7.0 %collective-permute-start.9 = (f32[4,16,256]{2,1,0:T(8,128)S(1)}, f32[4,16,256]{2,1,0:T(8,128)S(1)}, u32[]{:S(2)}, u32[]{:S(2)}) collective-permute-start(f32[4,16,256]{2,1,0:T(8,128)S(1)} %get-tuple-element.136), channel_id=1, source_target_pairs={{16,0},{32,16},{48,32},{64,48},{80,64},{96,80},{112,96},{128,112},... | collective-permute-start | bytes 196616 | tf_op jit(solution)/shard_map/ppermute | solution.py:25
  65.4 2.9 %collective-permute-start.10 = (f32[8,4,256]{2,1,0:T(4,128)S(1)}, f32[8,4,256]{2,1,0:T(4,128)S(1)}, u32[]{:S(2)}, u32[]{:S(2)}) collective-permute-start(f32[8,4,256]{2,1,0:T(4,128)S(1)} %get-tuple-element.138), channel_id=1, source_target_pairs={{1,0},{2,1},{3,2},{4,3},{5,4},{6,5},{7,6},{8,7},{9,8},{10,9},{11,1... | collective-permute-start | bytes 98312 | tf_op jit(solution)/shard_map/ppermute | solution.py:25
  68.4 2.3 %collective-permute-start.11 = (f32[8,4,256]{2,1,0:T(4,128)S(1)}, f32[8,4,256]{2,1,0:T(4,128)S(1)}, u32[]{:S(2)}, u32[]{:S(2)}) collective-permute-start(f32[8,4,256]{2,1,0:T(4,128)S(1)} %get-tuple-element.137), channel_id=1, source_target_pairs={{0,1},{1,2},{2,3},{3,4},{4,5},{5,6},{6,7},{7,8},{8,9},{9,10},{10,1... | collective-permute-start | bytes 98312 | tf_op jit(solution)/shard_map/ppermute | solution.py:24
  73.0 2.1 %collective-permute-done.11 = f32[8,4,256]{2,1,0:T(4,128)S(1)} collective-permute-done((f32[8,4,256]{2,1,0:T(4,128)S(1)}, f32[8,4,256]{2,1,0:T(4,128)S(1)}, u32[]{:S(2)}, u32[]{:S(2)}) %collective-permute-start.11) | collective-permute-done | bytes 32800 | tf_op jit(solution)/shard_map/ppermute | solution.py:24
  76.1 1.9 %collective-permute-start.12 = (f32[4,16,256]{2,1,0:T(8,128)S(1)}, f32[4,16,256]{2,1,0:T(8,128)S(1)}, u32[]{:S(2)}, u32[]{:S(2)}) collective-permute-start(f32[4,16,256]{2,1,0:T(8,128)S(1)} %get-tuple-element.131), channel_id=1, source_target_pairs={{0,16},{16,32},{32,48},{48,64},{64,80},{80,96},{96,112},{112,128},... | collective-permute-start | bytes 196616 | tf_op jit(solution)/shard_map/ppermute | solution.py:24
  78.0 7.0 %collective-permute-start.13 = (f32[4,16,256]{2,1,0:T(8,128)S(1)}, f32[4,16,256]{2,1,0:T(8,128)S(1)}, u32[]{:S(2)}, u32[]{:S(2)}) collective-permute-start(f32[4,16,256]{2,1,0:T(8,128)S(1)} %get-tuple-element.132), channel_id=1, source_target_pairs={{16,0},{32,16},{48,32},{64,48},{80,64},{96,80},{112,96},{128,112},... | collective-permute-start | bytes 196616 | tf_op jit(solution)/shard_map/ppermute | solution.py:25
  85.0 3.0 %collective-permute-start.14 = (f32[8,4,256]{2,1,0:T(4,128)S(1)}, f32[8,4,256]{2,1,0:T(4,128)S(1)}, u32[]{:S(2)}, u32[]{:S(2)}) collective-permute-start(f32[8,4,256]{2,1,0:T(4,128)S(1)} %get-tuple-element.134), channel_id=1, source_target_pairs={{1,0},{2,1},{3,2},{4,3},{5,4},{6,5},{7,6},{8,7},{9,8},{10,9},{11,1... | collective-permute-start | bytes 98312 | tf_op jit(solution)/shard_map/ppermute | solution.py:25
  88.0 2.3 %collective-permute-start.15 = (f32[8,4,256]{2,1,0:T(4,128)S(1)}, f32[8,4,256]{2,1,0:T(4,128)S(1)}, u32[]{:S(2)}, u32[]{:S(2)}) collective-permute-start(f32[8,4,256]{2,1,0:T(4,128)S(1)} %get-tuple-element.133), channel_id=1, source_target_pairs={{0,1},{1,2},{2,3},{3,4},{4,5},{5,6},{6,7},{7,8},{8,9},{9,10},{10,1... | collective-permute-start | bytes 98312 | tf_op jit(solution)/shard_map/ppermute | solution.py:24
  92.8 2.0 %collective-permute-done.15 = f32[8,4,256]{2,1,0:T(4,128)S(1)} collective-permute-done((f32[8,4,256]{2,1,0:T(4,128)S(1)}, f32[8,4,256]{2,1,0:T(4,128)S(1)}, u32[]{:S(2)}, u32[]{:S(2)}) %collective-permute-start.15) | collective-permute-done | bytes 32800 | tf_op jit(solution)/shard_map/ppermute | solution.py:24
  95.7 1.9 %collective-permute-start.17 = (f32[4,16,256]{2,1,0:T(8,128)S(1)}, f32[4,16,256]{2,1,0:T(8,128)S(1)}, u32[]{:S(2)}, u32[]{:S(2)}) collective-permute-start(f32[4,16,256]{2,1,0:T(8,128)S(1)} %get-tuple-element.127), channel_id=1, source_target_pairs={{0,16},{16,32},{32,48},{48,64},{64,80},{80,96},{96,112},{112,128},... | collective-permute-start | bytes 196616 | tf_op jit(solution)/shard_map/ppermute | solution.py:24
  97.7 7.0 %collective-permute-start.18 = (f32[4,16,256]{2,1,0:T(8,128)S(1)}, f32[4,16,256]{2,1,0:T(8,128)S(1)}, u32[]{:S(2)}, u32[]{:S(2)}) collective-permute-start(f32[4,16,256]{2,1,0:T(8,128)S(1)} %get-tuple-element.128), channel_id=1, source_target_pairs={{16,0},{32,16},{48,32},{64,48},{80,64},{96,80},{112,96},{128,112},... | collective-permute-start | bytes 196616 | tf_op jit(solution)/shard_map/ppermute | solution.py:25
  104.6 3.1 %collective-permute-start.19 = (f32[8,4,256]{2,1,0:T(4,128)S(1)}, f32[8,4,256]{2,1,0:T(4,128)S(1)}, u32[]{:S(2)}, u32[]{:S(2)}) collective-permute-start(f32[8,4,256]{2,1,0:T(4,128)S(1)} %get-tuple-element.130), channel_id=1, source_target_pairs={{1,0},{2,1},{3,2},{4,3},{5,4},{6,5},{7,6},{8,7},{9,8},{10,9},{11,1... | collective-permute-start | bytes 98312 | tf_op jit(solution)/shard_map/ppermute | solution.py:25
  107.7 2.2 %collective-permute-start.20 = (f32[8,4,256]{2,1,0:T(4,128)S(1)}, f32[8,4,256]{2,1,0:T(4,128)S(1)}, u32[]{:S(2)}, u32[]{:S(2)}) collective-permute-start(f32[8,4,256]{2,1,0:T(4,128)S(1)} %get-tuple-element.129), channel_id=1, source_target_pairs={{0,1},{1,2},{2,3},{3,4},{4,5},{5,6},{6,7},{7,8},{8,9},{9,10},{10,1... | collective-permute-start | bytes 98312 | tf_op jit(solution)/shard_map/ppermute | solution.py:24
  112.4 2.1 %collective-permute-done.20 = f32[8,4,256]{2,1,0:T(4,128)S(1)} collective-permute-done((f32[8,4,256]{2,1,0:T(4,128)S(1)}, f32[8,4,256]{2,1,0:T(4,128)S(1)}, u32[]{:S(2)}, u32[]{:S(2)}) %collective-permute-start.20) | collective-permute-done | bytes 32800 | tf_op jit(solution)/shard_map/ppermute | solution.py:24
  117.4 7.0 %collective-permute-start.22 = (f32[4,16,256]{2,1,0:T(8,128)S(1)}, f32[4,16,256]{2,1,0:T(8,128)S(1)}, u32[]{:S(2)}, u32[]{:S(2)}) collective-permute-start(f32[4,16,256]{2,1,0:T(8,128)S(1)} %get-tuple-element.124), channel_id=1, source_target_pairs={{16,0},{32,16},{48,32},{64,48},{80,64},{96,80},{112,96},{128,112},... | collective-permute-start | bytes 196616 | tf_op jit(solution)/shard_map/ppermute | solution.py:25
  124.4 3.1 %collective-permute-start.23 = (f32[8,4,256]{2,1,0:T(4,128)S(1)}, f32[8,4,256]{2,1,0:T(4,128)S(1)}, u32[]{:S(2)}, u32[]{:S(2)}) collective-permute-start(f32[8,4,256]{2,1,0:T(4,128)S(1)} %get-tuple-element.126), channel_id=1, source_target_pairs={{1,0},{2,1},{3,2},{4,3},{5,4},{6,5},{7,6},{8,7},{9,8},{10,9},{11,1... | collective-permute-start | bytes 98312 | tf_op jit(solution)/shard_map/ppermute | solution.py:25
  127.5 2.4 %collective-permute-start.24 = (f32[8,4,256]{2,1,0:T(4,128)S(1)}, f32[8,4,256]{2,1,0:T(4,128)S(1)}, u32[]{:S(2)}, u32[]{:S(2)}) collective-permute-start(f32[8,4,256]{2,1,0:T(4,128)S(1)} %get-tuple-element.125), channel_id=1, source_target_pairs={{0,1},{1,2},{2,3},{3,4},{4,5},{5,6},{6,7},{7,8},{8,9},{9,10},{10,1... | collective-permute-start | bytes 98312 | tf_op jit(solution)/shard_map/ppermute | solution.py:24
  132.2 2.3 %collective-permute-done.24 = f32[8,4,256]{2,1,0:T(4,128)S(1)} collective-permute-done((f32[8,4,256]{2,1,0:T(4,128)S(1)}, f32[8,4,256]{2,1,0:T(4,128)S(1)}, u32[]{:S(2)}, u32[]{:S(2)}) %collective-permute-start.24) | collective-permute-done | bytes 32800 | tf_op jit(solution)/shard_map/ppermute | solution.py:24
  137.3 7.0 %collective-permute-start.26 = (f32[4,16,256]{2,1,0:T(8,128)S(1)}, f32[4,16,256]{2,1,0:T(8,128)S(1)}, u32[]{:S(2)}, u32[]{:S(2)}) collective-permute-start(f32[4,16,256]{2,1,0:T(8,128)S(1)} %get-tuple-element.120), channel_id=1, source_target_pairs={{16,0},{32,16},{48,32},{64,48},{80,64},{96,80},{112,96},{128,112},... | collective-permute-start | bytes 196616 | tf_op jit(solution)/shard_map/ppermute | solution.py:25
  144.3 3.0 %collective-permute-start.27 = (f32[8,4,256]{2,1,0:T(4,128)S(1)}, f32[8,4,256]{2,1,0:T(4,128)S(1)}, u32[]{:S(2)}, u32[]{:S(2)}) collective-permute-start(f32[8,4,256]{2,1,0:T(4,128)S(1)} %get-tuple-element.122), channel_id=1, source_target_pairs={{1,0},{2,1},{3,2},{4,3},{5,4},{6,5},{7,6},{8,7},{9,8},{10,9},{11,1... | collective-permute-start | bytes 98312 | tf_op jit(solution)/shard_map/ppermute | solution.py:25
  147.3 2.3 %collective-permute-start.28 = (f32[8,4,256]{2,1,0:T(4,128)S(1)}, f32[8,4,256]{2,1,0:T(4,128)S(1)}, u32[]{:S(2)}, u32[]{:S(2)}) collective-permute-start(f32[8,4,256]{2,1,0:T(4,128)S(1)} %get-tuple-element.121), channel_id=1, source_target_pairs={{0,1},{1,2},{2,3},{3,4},{4,5},{5,6},{6,7},{7,8},{8,9},{9,10},{10,1... | collective-permute-start | bytes 98312 | tf_op jit(solution)/shard_map/ppermute | solution.py:24
  157.1 7.0 %collective-permute-start.30 = (f32[4,16,256]{2,1,0:T(8,128)S(1)}, f32[4,16,256]{2,1,0:T(8,128)S(1)}, u32[]{:S(2)}, u32[]{:S(2)}) collective-permute-start(f32[4,16,256]{2,1,0:T(8,128)S(1)} %get-tuple-element.116), channel_id=1, source_target_pairs={{16,0},{32,16},{48,32},{64,48},{80,64},{96,80},{112,96},{128,112},... | collective-permute-start | bytes 196616 | tf_op jit(solution)/shard_map/ppermute | solution.py:25
  164.1 5.1 %collective-permute-start.31 = (f32[8,4,256]{2,1,0:T(4,128)S(1)}, f32[8,4,256]{2,1,0:T(4,128)S(1)}, u32[]{:S(2)}, u32[]{:S(2)}) collective-permute-start(f32[8,4,256]{2,1,0:T(4,128)S(1)} %get-tuple-element.118), channel_id=1, source_target_pairs={{1,0},{2,1},{3,2},{4,3},{5,4},{6,5},{7,6},{8,7},{9,8},{10,9},{11,1... | collective-permute-start | bytes 98312 | tf_op jit(solution)/shard_map/ppermute | solution.py:25
  171.1 11.3 %collective-permute-start.16 = (f32[8,16,128]{2,1,0:T(8,128)S(1)}, f32[8,16,128]{2,1,0:T(8,128)S(1)}, u32[]{:S(2)}, u32[]{:S(2)}) collective-permute-start(f32[8,16,128]{2,1,0:T(8,128)S(1)} %slice_select_fusion.1), channel_id=1, source_target_pairs={{0,256},{256,0},{1,257},{257,1},{2,258},{258,2},{3,259},{259,3},{4... | collective-permute-start | bytes 196616 | tf_op jit(solution)/shard_map/ppermute | solution.py:13
  183.4 5.9 %collective-permute-start.33 = (f32[8,16,128]{2,1,0:T(8,128)S(1)}, f32[8,16,128]{2,1,0:T(8,128)S(1)}, u32[]{:S(2)}, u32[]{:S(2)}) collective-permute-start(f32[8,16,128]{2,1,0:T(8,128)S(1)} %slice_select_fusion), channel_id=1, source_target_pairs={{0,256},{256,0},{1,257},{257,1},{2,258},{258,2},{3,259},{259,3},{4... | collective-permute-start | bytes 196616 | tf_op jit(solution)/shard_map/ppermute | solution.py:13
  (199 shorter events, 41.2 us)
Async XLA Ops:
  1.6 31.1 %collective-permute-start.2 = (f32[8,4,256]{2,1,0:T(4,128)S(1)}, f32[8,4,256]{2,1,0:T(4,128)S(1)}, u32[]{:S(2)}, u32[]{:S(2)}) collective-permute-start(f32[8,4,256]{2,1,0:T(4,128)S(1)} %get-tuple-element.146), channel_id=1, source_target_pairs={{1,0},{2,1},{3,2},{4,3},{5,4},{6,5},{7,6},{8,7},{9,8},{10,9},{11,1... | collective-permute-start | bytes 98312 | tf_op jit(solution)/shard_map/ppermute | solution.py:25
  12.5 20.1 %collective-permute-start.3 = (f32[8,4,256]{2,1,0:T(4,128)S(1)}, f32[8,4,256]{2,1,0:T(4,128)S(1)}, u32[]{:S(2)}, u32[]{:S(2)}) collective-permute-start(f32[8,4,256]{2,1,0:T(4,128)S(1)} %get-tuple-element.145), channel_id=1, source_target_pairs={{0,1},{1,2},{2,3},{3,4},{4,5},{5,6},{6,7},{7,8},{8,9},{9,10},{10,1... | collective-permute-start | bytes 98312 | tf_op jit(solution)/shard_map/ppermute | solution.py:24
  14.6 18.1 %collective-permute-start = (f32[4,16,256]{2,1,0:T(8,128)S(1)}, f32[4,16,256]{2,1,0:T(8,128)S(1)}, u32[]{:S(2)}, u32[]{:S(2)}) collective-permute-start(f32[4,16,256]{2,1,0:T(8,128)S(1)} %get-tuple-element.143), channel_id=1, source_target_pairs={{0,16},{16,32},{32,48},{48,64},{64,80},{80,96},{96,112},{112,128},... | collective-permute-start | bytes 196616 | tf_op jit(solution)/shard_map/ppermute | solution.py:24
  17.8 14.9 %collective-permute-start.1 = (f32[4,16,256]{2,1,0:T(8,128)S(1)}, f32[4,16,256]{2,1,0:T(8,128)S(1)}, u32[]{:S(2)}, u32[]{:S(2)}) collective-permute-start(f32[4,16,256]{2,1,0:T(8,128)S(1)} %get-tuple-element.144), channel_id=1, source_target_pairs={{16,0},{32,16},{48,32},{64,48},{80,64},{96,80},{112,96},{128,112},... | collective-permute-start | bytes 196616 | tf_op jit(solution)/shard_map/ppermute | solution.py:25
  34.3 21.2 %collective-permute-start.4 = (f32[4,16,256]{2,1,0:T(8,128)S(1)}, f32[4,16,256]{2,1,0:T(8,128)S(1)}, u32[]{:S(2)}, u32[]{:S(2)}) collective-permute-start(f32[4,16,256]{2,1,0:T(8,128)S(1)} %get-tuple-element.139), channel_id=1, source_target_pairs={{0,16},{16,32},{32,48},{48,64},{64,80},{80,96},{96,112},{112,128},... | collective-permute-start | bytes 196616 | tf_op jit(solution)/shard_map/ppermute | solution.py:24
  36.3 19.3 %collective-permute-start.5 = (f32[4,16,256]{2,1,0:T(8,128)S(1)}, f32[4,16,256]{2,1,0:T(8,128)S(1)}, u32[]{:S(2)}, u32[]{:S(2)}) collective-permute-start(f32[4,16,256]{2,1,0:T(8,128)S(1)} %get-tuple-element.140), channel_id=1, source_target_pairs={{16,0},{32,16},{48,32},{64,48},{80,64},{96,80},{112,96},{128,112},... | collective-permute-start | bytes 196616 | tf_op jit(solution)/shard_map/ppermute | solution.py:25
  43.3 9.7 %collective-permute-start.6 = (f32[8,4,256]{2,1,0:T(4,128)S(1)}, f32[8,4,256]{2,1,0:T(4,128)S(1)}, u32[]{:S(2)}, u32[]{:S(2)}) collective-permute-start(f32[8,4,256]{2,1,0:T(4,128)S(1)} %get-tuple-element.142), channel_id=1, source_target_pairs={{1,0},{2,1},{3,2},{4,3},{5,4},{6,5},{7,6},{8,7},{9,8},{10,9},{11,1... | collective-permute-start | bytes 98312 | tf_op jit(solution)/shard_map/ppermute | solution.py:25
  48.7 6.8 %collective-permute-start.7 = (f32[8,4,256]{2,1,0:T(4,128)S(1)}, f32[8,4,256]{2,1,0:T(4,128)S(1)}, u32[]{:S(2)}, u32[]{:S(2)}) collective-permute-start(f32[8,4,256]{2,1,0:T(4,128)S(1)} %get-tuple-element.141), channel_id=1, source_target_pairs={{0,1},{1,2},{2,3},{3,4},{4,5},{5,6},{6,7},{7,8},{8,9},{9,10},{10,1... | collective-permute-start | bytes 98312 | tf_op jit(solution)/shard_map/ppermute | solution.py:24
  56.5 18.7 %collective-permute-start.8 = (f32[4,16,256]{2,1,0:T(8,128)S(1)}, f32[4,16,256]{2,1,0:T(8,128)S(1)}, u32[]{:S(2)}, u32[]{:S(2)}) collective-permute-start(f32[4,16,256]{2,1,0:T(8,128)S(1)} %get-tuple-element.135), channel_id=1, source_target_pairs={{0,16},{16,32},{32,48},{48,64},{64,80},{80,96},{96,112},{112,128},... | collective-permute-start | bytes 196616 | tf_op jit(solution)/shard_map/ppermute | solution.py:24
  58.4 16.7 %collective-permute-start.9 = (f32[4,16,256]{2,1,0:T(8,128)S(1)}, f32[4,16,256]{2,1,0:T(8,128)S(1)}, u32[]{:S(2)}, u32[]{:S(2)}) collective-permute-start(f32[4,16,256]{2,1,0:T(8,128)S(1)} %get-tuple-element.136), channel_id=1, source_target_pairs={{16,0},{32,16},{48,32},{64,48},{80,64},{96,80},{112,96},{128,112},... | collective-permute-start | bytes 196616 | tf_op jit(solution)/shard_map/ppermute | solution.py:25
  65.4 7.6 %collective-permute-start.10 = (f32[8,4,256]{2,1,0:T(4,128)S(1)}, f32[8,4,256]{2,1,0:T(4,128)S(1)}, u32[]{:S(2)}, u32[]{:S(2)}) collective-permute-start(f32[8,4,256]{2,1,0:T(4,128)S(1)} %get-tuple-element.138), channel_id=1, source_target_pairs={{1,0},{2,1},{3,2},{4,3},{5,4},{6,5},{7,6},{8,7},{9,8},{10,9},{11,1... | collective-permute-start | bytes 98312 | tf_op jit(solution)/shard_map/ppermute | solution.py:25
  68.4 6.8 %collective-permute-start.11 = (f32[8,4,256]{2,1,0:T(4,128)S(1)}, f32[8,4,256]{2,1,0:T(4,128)S(1)}, u32[]{:S(2)}, u32[]{:S(2)}) collective-permute-start(f32[8,4,256]{2,1,0:T(4,128)S(1)} %get-tuple-element.137), channel_id=1, source_target_pairs={{0,1},{1,2},{2,3},{3,4},{4,5},{5,6},{6,7},{7,8},{8,9},{9,10},{10,1... | collective-permute-start | bytes 98312 | tf_op jit(solution)/shard_map/ppermute | solution.py:24
  76.1 18.7 %collective-permute-start.12 = (f32[4,16,256]{2,1,0:T(8,128)S(1)}, f32[4,16,256]{2,1,0:T(8,128)S(1)}, u32[]{:S(2)}, u32[]{:S(2)}) collective-permute-start(f32[4,16,256]{2,1,0:T(8,128)S(1)} %get-tuple-element.131), channel_id=1, source_target_pairs={{0,16},{16,32},{32,48},{48,64},{64,80},{80,96},{96,112},{112,128},... | collective-permute-start | bytes 196616 | tf_op jit(solution)/shard_map/ppermute | solution.py:24
  78.0 16.7 %collective-permute-start.13 = (f32[4,16,256]{2,1,0:T(8,128)S(1)}, f32[4,16,256]{2,1,0:T(8,128)S(1)}, u32[]{:S(2)}, u32[]{:S(2)}) collective-permute-start(f32[4,16,256]{2,1,0:T(8,128)S(1)} %get-tuple-element.132), channel_id=1, source_target_pairs={{16,0},{32,16},{48,32},{64,48},{80,64},{96,80},{112,96},{128,112},... | collective-permute-start | bytes 196616 | tf_op jit(solution)/shard_map/ppermute | solution.py:25
  85.0 7.7 %collective-permute-start.14 = (f32[8,4,256]{2,1,0:T(4,128)S(1)}, f32[8,4,256]{2,1,0:T(4,128)S(1)}, u32[]{:S(2)}, u32[]{:S(2)}) collective-permute-start(f32[8,4,256]{2,1,0:T(4,128)S(1)} %get-tuple-element.134), channel_id=1, source_target_pairs={{1,0},{2,1},{3,2},{4,3},{5,4},{6,5},{7,6},{8,7},{9,8},{10,9},{11,1... | collective-permute-start | bytes 98312 | tf_op jit(solution)/shard_map/ppermute | solution.py:25
  95.7 18.8 %collective-permute-start.17 = (f32[4,16,256]{2,1,0:T(8,128)S(1)}, f32[4,16,256]{2,1,0:T(8,128)S(1)}, u32[]{:S(2)}, u32[]{:S(2)}) collective-permute-start(f32[4,16,256]{2,1,0:T(8,128)S(1)} %get-tuple-element.127), channel_id=1, source_target_pairs={{0,16},{16,32},{32,48},{48,64},{64,80},{80,96},{96,112},{112,128},... | collective-permute-start | bytes 196616 | tf_op jit(solution)/shard_map/ppermute | solution.py:24
  97.7 16.9 %collective-permute-start.18 = (f32[4,16,256]{2,1,0:T(8,128)S(1)}, f32[4,16,256]{2,1,0:T(8,128)S(1)}, u32[]{:S(2)}, u32[]{:S(2)}) collective-permute-start(f32[4,16,256]{2,1,0:T(8,128)S(1)} %get-tuple-element.128), channel_id=1, source_target_pairs={{16,0},{32,16},{48,32},{64,48},{80,64},{96,80},{112,96},{128,112},... | collective-permute-start | bytes 196616 | tf_op jit(solution)/shard_map/ppermute | solution.py:25
  104.6 7.7 %collective-permute-start.19 = (f32[8,4,256]{2,1,0:T(4,128)S(1)}, f32[8,4,256]{2,1,0:T(4,128)S(1)}, u32[]{:S(2)}, u32[]{:S(2)}) collective-permute-start(f32[8,4,256]{2,1,0:T(4,128)S(1)} %get-tuple-element.130), channel_id=1, source_target_pairs={{1,0},{2,1},{3,2},{4,3},{5,4},{6,5},{7,6},{8,7},{9,8},{10,9},{11,1... | collective-permute-start | bytes 98312 | tf_op jit(solution)/shard_map/ppermute | solution.py:25
  115.5 19.0 %collective-permute-start.21 = (f32[4,16,256]{2,1,0:T(8,128)S(1)}, f32[4,16,256]{2,1,0:T(8,128)S(1)}, u32[]{:S(2)}, u32[]{:S(2)}) collective-permute-start(f32[4,16,256]{2,1,0:T(8,128)S(1)} %get-tuple-element.123), channel_id=1, source_target_pairs={{0,16},{16,32},{32,48},{48,64},{64,80},{80,96},{96,112},{112,128},... | collective-permute-start | bytes 196616 | tf_op jit(solution)/shard_map/ppermute | solution.py:24
  117.4 17.1 %collective-permute-start.22 = (f32[4,16,256]{2,1,0:T(8,128)S(1)}, f32[4,16,256]{2,1,0:T(8,128)S(1)}, u32[]{:S(2)}, u32[]{:S(2)}) collective-permute-start(f32[4,16,256]{2,1,0:T(8,128)S(1)} %get-tuple-element.124), channel_id=1, source_target_pairs={{16,0},{32,16},{48,32},{64,48},{80,64},{96,80},{112,96},{128,112},... | collective-permute-start | bytes 196616 | tf_op jit(solution)/shard_map/ppermute | solution.py:25
  124.4 7.8 %collective-permute-start.23 = (f32[8,4,256]{2,1,0:T(4,128)S(1)}, f32[8,4,256]{2,1,0:T(4,128)S(1)}, u32[]{:S(2)}, u32[]{:S(2)}) collective-permute-start(f32[8,4,256]{2,1,0:T(4,128)S(1)} %get-tuple-element.126), channel_id=1, source_target_pairs={{1,0},{2,1},{3,2},{4,3},{5,4},{6,5},{7,6},{8,7},{9,8},{10,9},{11,1... | collective-permute-start | bytes 98312 | tf_op jit(solution)/shard_map/ppermute | solution.py:25
  127.5 6.9 %collective-permute-start.24 = (f32[8,4,256]{2,1,0:T(4,128)S(1)}, f32[8,4,256]{2,1,0:T(4,128)S(1)}, u32[]{:S(2)}, u32[]{:S(2)}) collective-permute-start(f32[8,4,256]{2,1,0:T(4,128)S(1)} %get-tuple-element.125), channel_id=1, source_target_pairs={{0,1},{1,2},{2,3},{3,4},{4,5},{5,6},{6,7},{7,8},{8,9},{9,10},{10,1... | collective-permute-start | bytes 98312 | tf_op jit(solution)/shard_map/ppermute | solution.py:24
  135.4 18.8 %collective-permute-start.25 = (f32[4,16,256]{2,1,0:T(8,128)S(1)}, f32[4,16,256]{2,1,0:T(8,128)S(1)}, u32[]{:S(2)}, u32[]{:S(2)}) collective-permute-start(f32[4,16,256]{2,1,0:T(8,128)S(1)} %get-tuple-element.119), channel_id=1, source_target_pairs={{0,16},{16,32},{32,48},{48,64},{64,80},{80,96},{96,112},{112,128},... | collective-permute-start | bytes 196616 | tf_op jit(solution)/shard_map/ppermute | solution.py:24
  137.3 16.8 %collective-permute-start.26 = (f32[4,16,256]{2,1,0:T(8,128)S(1)}, f32[4,16,256]{2,1,0:T(8,128)S(1)}, u32[]{:S(2)}, u32[]{:S(2)}) collective-permute-start(f32[4,16,256]{2,1,0:T(8,128)S(1)} %get-tuple-element.120), channel_id=1, source_target_pairs={{16,0},{32,16},{48,32},{64,48},{80,64},{96,80},{112,96},{128,112},... | collective-permute-start | bytes 196616 | tf_op jit(solution)/shard_map/ppermute | solution.py:25
  144.3 9.8 %collective-permute-start.27 = (f32[8,4,256]{2,1,0:T(4,128)S(1)}, f32[8,4,256]{2,1,0:T(4,128)S(1)}, u32[]{:S(2)}, u32[]{:S(2)}) collective-permute-start(f32[8,4,256]{2,1,0:T(4,128)S(1)} %get-tuple-element.122), channel_id=1, source_target_pairs={{1,0},{2,1},{3,2},{4,3},{5,4},{6,5},{7,6},{8,7},{9,8},{10,9},{11,1... | collective-permute-start | bytes 98312 | tf_op jit(solution)/shard_map/ppermute | solution.py:25
  147.3 6.8 %collective-permute-start.28 = (f32[8,4,256]{2,1,0:T(4,128)S(1)}, f32[8,4,256]{2,1,0:T(4,128)S(1)}, u32[]{:S(2)}, u32[]{:S(2)}) collective-permute-start(f32[8,4,256]{2,1,0:T(4,128)S(1)} %get-tuple-element.121), channel_id=1, source_target_pairs={{0,1},{1,2},{2,3},{3,4},{4,5},{5,6},{6,7},{7,8},{8,9},{9,10},{10,1... | collective-permute-start | bytes 98312 | tf_op jit(solution)/shard_map/ppermute | solution.py:24
  155.1 27.3 %collective-permute-start.29 = (f32[4,16,256]{2,1,0:T(8,128)S(1)}, f32[4,16,256]{2,1,0:T(8,128)S(1)}, u32[]{:S(2)}, u32[]{:S(2)}) collective-permute-start(f32[4,16,256]{2,1,0:T(8,128)S(1)} %get-tuple-element.115), channel_id=1, source_target_pairs={{0,16},{16,32},{32,48},{48,64},{64,80},{80,96},{96,112},{112,128},... | collective-permute-start | bytes 196616 | tf_op jit(solution)/shard_map/ppermute | solution.py:24
  157.1 25.4 %collective-permute-start.30 = (f32[4,16,256]{2,1,0:T(8,128)S(1)}, f32[4,16,256]{2,1,0:T(8,128)S(1)}, u32[]{:S(2)}, u32[]{:S(2)}) collective-permute-start(f32[4,16,256]{2,1,0:T(8,128)S(1)} %get-tuple-element.116), channel_id=1, source_target_pairs={{16,0},{32,16},{48,32},{64,48},{80,64},{96,80},{112,96},{128,112},... | collective-permute-start | bytes 196616 | tf_op jit(solution)/shard_map/ppermute | solution.py:25
  164.1 18.3 %collective-permute-start.31 = (f32[8,4,256]{2,1,0:T(4,128)S(1)}, f32[8,4,256]{2,1,0:T(4,128)S(1)}, u32[]{:S(2)}, u32[]{:S(2)}) collective-permute-start(f32[8,4,256]{2,1,0:T(4,128)S(1)} %get-tuple-element.118), channel_id=1, source_target_pairs={{1,0},{2,1},{3,2},{4,3},{5,4},{6,5},{7,6},{8,7},{9,8},{10,9},{11,1... | collective-permute-start | bytes 98312 | tf_op jit(solution)/shard_map/ppermute | solution.py:25
  169.1 13.3 %collective-permute-start.32 = (f32[8,4,256]{2,1,0:T(4,128)S(1)}, f32[8,4,256]{2,1,0:T(4,128)S(1)}, u32[]{:S(2)}, u32[]{:S(2)}) collective-permute-start(f32[8,4,256]{2,1,0:T(4,128)S(1)} %get-tuple-element.117), channel_id=1, source_target_pairs={{0,1},{1,2},{2,3},{3,4},{4,5},{5,6},{6,7},{7,8},{8,9},{9,10},{10,1... | collective-permute-start | bytes 98312 | tf_op jit(solution)/shard_map/ppermute | solution.py:24
  171.1 18.2 %collective-permute-start.16 = (f32[8,16,128]{2,1,0:T(8,128)S(1)}, f32[8,16,128]{2,1,0:T(8,128)S(1)}, u32[]{:S(2)}, u32[]{:S(2)}) collective-permute-start(f32[8,16,128]{2,1,0:T(8,128)S(1)} %slice_select_fusion.1), channel_id=1, source_target_pairs={{0,256},{256,0},{1,257},{257,1},{2,258},{258,2},{3,259},{259,3},{4... | collective-permute-start | bytes 196616 | tf_op jit(solution)/shard_map/ppermute | solution.py:13
  183.4 6.8 %collective-permute-start.33 = (f32[8,16,128]{2,1,0:T(8,128)S(1)}, f32[8,16,128]{2,1,0:T(8,128)S(1)}, u32[]{:S(2)}, u32[]{:S(2)}) collective-permute-start(f32[8,16,128]{2,1,0:T(8,128)S(1)} %slice_select_fusion), channel_id=1, source_target_pairs={{0,256},{256,0},{1,257},{257,1},{2,258},{258,2},{3,259},{259,3},{4... | collective-permute-start | bytes 196616 | tf_op jit(solution)/shard_map/ppermute | solution.py:13
  (12 other events, 85.3 us)
where the time goes:
time: 192 us; the launch traced here: 191 us
  starting transfers between devices  142 us (74%)
  other arithmetic  18 us (9%)
  waiting for transfers between devices  12 us (6%)
  between operations  9.75 us (5%)
  local copies, waits for them, and re-layouts  8.78 us (5%)
    ppermute x16, starting transfers between devices, extended(): lax.ppermute(initial, axis, [(b, a) for a, b in up])  91 us
    ppermute x16, starting transfers between devices, extended(): lax.ppermute(last, axis, up)  34.1 us
    ppermute x2, starting transfers between devices, from_partner(): lax.ppermute(shard, axis, [(i, i ^ 1 << bit) for i in range(lax.axis_size...  17.2 us
    ppermute x16, waiting for transfers between devices, extended(): lax.ppermute(last, axis, up)  11.1 us
    scatter-add x8, other arithmetic, local(): receiver_add = jnp.zeros((total_cells,), jnp.float32).at[flat_cells].add(...  10.3 us
  transfers between devices with their start and end apart: 34, of which 6 were waited for; matrix products, arithmetic and copies ran while one was open for 9% of the time, Pallas kernels for 0%

commit v1 on v0

v1 whole, which is shorter than its diff:
```python
import jax
import jax.numpy as jnp
from jax import lax
from jax.experimental import pallas as pl
from jax.experimental.pallas import tpu as pltpu
from jax.sharding import PartitionSpec as P

STEPS = 8
STENCIL = (-205.0 / 72.0, 8.0 / 5.0, -1.0 / 5.0, 8.0 / 315.0, -1.0 / 560.0)
MESH = pl.DeviceIdType.MESH
F32 = jnp.float32
BF16 = jnp.bfloat16


def split3(value):
    high = value.astype(BF16).astype(F32)
    rest = value - high
    middle = rest.astype(BF16).astype(F32)
    return high, middle, rest - middle


def shifted_sum(lower, upper, k, lane):
    lower_up, upper_up = pltpu.roll(lower, k, 1), pltpu.roll(upper, k, 1)
    lower_down, upper_down = pltpu.roll(lower, 128 - k, 1), pltpu.roll(upper, 128 - k, 1)
    zero = jnp.zeros_like(lower)
    first, last = lane >= k, lane < 128 - k
    return (
        jnp.where(first, lower_up, zero) + jnp.where(last, lower_down, upper_down),
        jnp.where(first, upper_up, lower_up) + jnp.where(last, upper_down, zero),
    )


def kernel(
    now, later, courant, strips, traces, cells, source, wavelet,
    image_out, now_out, later_out,
    u, xr, yr, ys, yl, yh, c, t, acc_inj, dense, image_in, image, strip_v, trace_v, cell_v,
    load_sem, xs_sem, xr_sem, ysend_sem, yr_sem, im_send, im_recv, out_sem,
):
    a0, a1, a2, a3, a4 = STENCIL
    weights = (a1, a2, a3, a4)
    group = lax.axis_index("grp")
    at_x = lax.axis_index("gx")
    at_y = lax.axis_index("gy")
    size_x = lax.axis_size("gx")
    size_y = lax.axis_size("gy")
    source_side = group == 0
    has_x = (at_x > 0, at_x < size_x - 1)
    has_y = (at_y > 0, at_y < size_y - 1)
    to_x = ({"gx": at_x - 1}, {"gx": at_x + 1})
    to_y = ({"gy": at_y - 1}, {"gy": at_y + 1})
    partner = {"grp": 1 - group}

    loads = []
    for h in range(2):
        zs = pl.ds(128 * h, 128)
        loads.append(pltpu.make_async_copy(now.at[0, :, :, zs], u.at[0, h, :, pl.ds(8, 16)], load_sem.at[h]))
        loads.append(pltpu.make_async_copy(later.at[0, :, :, zs], u.at[1, h, :, pl.ds(8, 16)], load_sem.at[2 + h]))
        loads.append(pltpu.make_async_copy(courant.at[:, :, zs], c.at[h], load_sem.at[4 + h]))
    loads.append(pltpu.make_async_copy(strips, strip_v, load_sem.at[6]))
    loads.append(pltpu.make_async_copy(traces, trace_v, load_sem.at[7]))
    loads.append(pltpu.make_async_copy(cells, cell_v, load_sem.at[8]))
    for copy in loads:
        copy.start()

    zero8 = jnp.zeros((2, 2, 8, 8, 128), F32)
    u[:, :, :, 0:8] = zero8
    u[:, :, :, 24:32] = zero8
    xr[...] = jnp.zeros_like(xr)
    yr[...] = jnp.zeros_like(yr)
    yl[...] = jnp.zeros_like(yl)
    yh[...] = jnp.zeros_like(yh)

    barrier = pltpu.get_barrier_semaphore()
    count = jnp.int32(1)
    pl.semaphore_signal(barrier, inc=1, device_id=partner, device_id_type=MESH)
    for d in range(2):
        count = count + has_x[d].astype(jnp.int32) + has_y[d].astype(jnp.int32)

        @pl.when(has_x[d])
        def _():
            pl.semaphore_signal(barrier, inc=1, device_id=to_x[d], device_id_type=MESH)

        @pl.when(has_y[d])
        def _():
            pl.semaphore_signal(barrier, inc=1, device_id=to_y[d], device_id_type=MESH)

    pl.semaphore_wait(barrier, count)

    def x_copy(par, d):
        return pltpu.make_async_remote_copy(
            src_ref=u.at[par, :, pl.ds(4 * d, 4), pl.ds(8, 16)],
            dst_ref=xr.at[par, 1 - d],
            send_sem=xs_sem.at[par, d],
            recv_sem=xr_sem.at[par, 1 - d],
            device_id=to_x[d],
            device_id_type=MESH,
        )

    def y_copy(par, d):
        return pltpu.make_async_remote_copy(
            src_ref=ys.at[par, d],
            dst_ref=yr.at[par, 1 - d],
            send_sem=ysend_sem.at[par, d],
            recv_sem=yr_sem.at[par, 1 - d],
            device_id=to_y[d],
            device_id_type=MESH,
        )

    def image_copy(slot):
        par = 0
        return pltpu.make_async_remote_copy(
            src_ref=u.at[par, 1 - group, :, pl.ds(8, 16)],
            dst_ref=image_in.at[slot],
            send_sem=im_send.at[slot],
            recv_sem=im_recv.at[slot],
            device_id=partner,
            device_id_type=MESH,
        )

    for copy in loads[:2] + loads[3:5]:
        pass
    loads[0].wait()
    loads[3].wait()
    for d in range(2):

        @pl.when(has_x[d])
        def _():
            x_copy(0, d).start()

    for d in range(2):
        ys[0, d] = u[0, :, :, 8 + 12 * d : 12 + 12 * d]

        @pl.when(has_y[d])
        def _():
            y_copy(0, d).start()

    for i in (1, 2, 4, 5, 6, 7, 8):
        loads[i].wait()

    lane = lax.broadcasted_iota(jnp.int32, (16, 128), 1)
    lane1 = lax.broadcasted_iota(jnp.int32, (1, 128), 1)
    source_x = source[0] - at_x * 8
    source_y = source[1] - at_y * 16
    inside = (source_x >= 0) & (source_x < 8) & (source_y >= 0) & (source_y < 16)
    source_flat = jnp.where(inside, (source_x * 16 + source_y) * 256 + source[2], -1)
    where_to = jnp.where(source_side, jnp.where(lane1 == 0, source_flat, -1), cell_v[0])
    row_of = jnp.where(where_to < 0, -1, ((where_to >> 7) & 1) * 128 + (where_to >> 8))
    column_of = where_to & 127
    column_hot = jnp.where(
        lax.broadcasted_iota(jnp.int32, (128, 128), 0) == column_of, 1.0, 0.0
    ).astype(BF16)
    row_hot = lax.broadcasted_iota(jnp.int32, (256, 128), 0) == row_of
    from_entry = lax.broadcasted_iota(jnp.int32, (128, 256), 0)
    to_depth = lax.broadcasted_iota(jnp.int32, (128, 256), 1)
    layer = from_entry & 7
    depth_of = jnp.where(layer < 4, layer, 248 + layer)
    spread = jnp.where(to_depth == depth_of, 1.0, 0.0).astype(BF16)
    own_row = (
        lax.broadcasted_iota(jnp.int32, (8, 16, 128), 2) >> 3
        == lax.broadcasted_iota(jnp.int32, (8, 16, 128), 1)
    )
    overwrite = (
        jnp.logical_and(lane < 4, source_side),
        jnp.logical_and(lane >= 124, source_side),
    )

    def prepare(par, k):
        sample = jnp.where(
            source_side, jnp.where(lane1 == 0, -wavelet[k], 0.0), trace_v[k, 0]
        )
        inject = jnp.zeros((256, 128), F32)
        for part in split3(sample):
            left = jnp.where(row_hot, part, 0.0).astype(BF16)
            inject = inject + lax.dot_general(
                left, column_hot, (((1,), (1,)), ((), ())), preferred_element_type=F32
            )
        acc_inj[...] = inject.reshape(2, 8, 16, 128)
        strip = jnp.zeros((128, 256), F32)
        for part in split3(strip_v[k]):
            left = jnp.where(own_row, part[:, None, :], 0.0).reshape(128, 128).astype(BF16)
            strip = strip + jnp.dot(left, spread, preferred_element_type=F32)
        for h in range(2):
            dense[h] = strip[:, 128 * h : 128 * h + 128].reshape(8, 16, 128)

        for x in range(8):
            for h in range(2):
                own = u[par, h, x, 8:24]
                total = acc_inj[h, x] + (3.0 * a0) * own
                for k_ in range(1, 5):
                    near = u[par, h, x, 8 - k_ : 24 - k_] + u[par, h, x, 8 + k_ : 24 + k_]
                    if x - k_ >= 0:
                        near = near + u[par, h, x - k_, 8:24]
                    if x + k_ < 8:
                        near = near + u[par, h, x + k_, 8:24]
                    total = total + weights[k_ - 1] * near
                acc_inj[h, x] = total
            lower, upper = u[par, 0, x, 8:24], u[par, 1, x, 8:24]
            sums = [acc_inj[0, x], acc_inj[1, x]]
            for k_ in range(1, 5):
                both = shifted_sum(lower, upper, k_, lane)
                for h in range(2):
                    sums[h] = sums[h] + weights[k_ - 1] * both[h]
            for h in range(2):
                value = 2.0 * (lower, upper)[h] - u[1 - par, h, x, 8:24] + c[h, x] * sums[h]
                t[h, x] = jnp.where(overwrite[h], dense[h, x], value)

    for x in range(8):
        for h in range(2):
            pass

    def y_halo(par, x, h):
        low = jnp.zeros((8, 128), F32)
        high = jnp.zeros((8, 128), F32)
        for m in range(4):
            low = low + weights[3 - m] * yl[h, x, m : m + 8]
            high = high + weights[3 - m] * yh[h, x, 4 - m : 12 - m]
        return low, high

    def finish(par, k, more):
        for d in range(2):

            @pl.when(has_y[d])
            def _():
                y_copy(par, 1 - d).wait_recv()

        for x in range(8):
            yl[:, x, 0:4] = yr[par, 0, :, x]
            yh[:, x, 8:12] = yr[par, 1, :, x]

        new = 1 - par
        for d in range(2):

            @pl.when(has_x[d])
            def _():
                x_copy(par, 1 - d).wait_recv()

            for x in range(4 * d, 4 * d + 4):
                for h in range(2):
                    extra = None
                    for j in range(4):
                        distance = x + 4 - j if d == 0 else 8 + j - x
                        if distance <= 4:
                            term = weights[distance - 1] * xr[par, d, h, j]
                            extra = term if extra is None else extra + term
                    low, high = y_halo(par, x, h)
                    cx = jnp.where(overwrite[h], 0.0, c[h, x])
                    first = t[h, x, 0:8] + cx[0:8] * (extra[0:8] + low)
                    second = t[h, x, 8:16] + cx[8:16] * (extra[8:16] + high)
                    u[new, h, x, 8:16] = first
                    u[new, h, x, 16:24] = second
                    ys[new, 0, h, x] = first[0:4]
                    ys[new, 1, h, x] = second[4:8]

            @pl.when(jnp.logical_and(more, has_x[d]))
            def _():
                x_copy(new, d).start()

        for d in range(2):

            @pl.when(jnp.logical_and(more, has_y[d]))
            def _():
                y_copy(new, d).start()

    def sent(par):
        for d in range(2):

            @pl.when(has_x[d])
            def _():
                x_copy(par, d).wait_send()

            @pl.when(has_y[d])
            def _():
                y_copy(par, d).wait_send()

    def four(half, carry):
        for s in range(4):
            k = 4 * half + s
            par = s % 2
            if s == 0:

                @pl.when(half == 1)
                def _():
                    image_copy(0).wait()
                    image[...] = u[0, group, :, 8:24] * image_in[0]

            prepare(par, k)
            if s == 0:

                @pl.when(half == 1)
                def _():
                    sent(1)

            else:
                sent(1 - par)
            finish(par, k, True if s < 3 else half == 0)
            if s == 3:

                @pl.when(half == 0)
                def _():
                    image_copy(0).start()

                @pl.when(half == 1)
                def _():
                    image_copy(1).start()

        return carry

    lax.fori_loop(0, 2, four, 0)
    outs = []
    for h in range(2):
        zs = pl.ds(128 * h, 128)
        outs.append(pltpu.make_async_copy(u.at[1, h, :, pl.ds(8, 16)], later_out.at[0, :, :, zs], out_sem.at[h]))
        outs.append(pltpu.make_async_copy(u.at[0, h, :, pl.ds(8, 16)], now_out.at[0, :, :, zs], out_sem.at[2 + h]))
    for copy in outs:
        copy.start()
    sent(1)
    image_copy(1).wait()
    image[...] = image[...] + u[0, group, :, 8:24] * image_in[1]
    last = pltpu.make_async_copy(image, image_out, out_sem.at[4])
    last.start()
    for copy in outs:
        copy.wait()
    last.wait()


def local(state_now, state_later, courant, strips, traces, receiver_cells, source_point, wavelet):
    any_space = pl.BlockSpec(memory_space=pl.ANY)
    smem = pl.BlockSpec(memory_space=pltpu.SMEM)
    dma = pltpu.SemaphoreType.DMA
    return pl.pallas_call(
        kernel,
        out_shape=(
            jax.ShapeDtypeStruct((8, 16, 128), F32),
            jax.ShapeDtypeStruct((1, 8, 16, 256), F32),
            jax.ShapeDtypeStruct((1, 8, 16, 256), F32),
        ),
        in_specs=[any_space] * 6 + [smem] * 2,
        out_specs=(any_space,) * 3,
        scratch_shapes=[
            pltpu.VMEM((2, 2, 8, 32, 128), F32),
            pltpu.VMEM((2, 2, 2, 4, 16, 128), F32),
            pltpu.VMEM((2, 2, 2, 8, 4, 128), F32),
            pltpu.VMEM((2, 2, 2, 8, 4, 128), F32),
            pltpu.VMEM((2, 8, 16, 128), F32),
            pltpu.VMEM((2, 8, 16, 128), F32),
            pltpu.VMEM((2, 8, 16, 128), F32),
            pltpu.VMEM((2, 8, 16, 128), F32),
            pltpu.VMEM((2, 8, 16, 128), F32),
            pltpu.VMEM((2, 8, 16, 128), F32),
            pltpu.VMEM((2, 8, 16, 128), F32),
            pltpu.VMEM((8, 16, 128), F32),
            pltpu.VMEM((8, 8, 128), F32),
            pltpu.VMEM((8, 1, 1, 128), F32),
            pltpu.VMEM((1, 1, 128), jnp.int32),
            dma((9,)),
            dma((2, 2)),
            dma((2, 2)),
            dma((2, 2)),
            dma((2, 2)),
            dma((2,)),
            dma((2,)),
            dma((5,)),
        ],
        compiler_params=pltpu.CompilerParams(collective_id=0, has_side_effects=True),
    )(state_now, state_later, courant, strips, traces, receiver_cells, source_point, wavelet)


def solution(mesh):
    in_specs = (
        P("grp", "gx", "gy", None),
        P("grp", "gx", "gy", None),
        P("gx", "gy", None),
        P(None, "gx", "gy"),
        P(None, "gx", "gy", None),
        P("gx", "gy", None),
        P(),
        P(),
    )
    out_specs = (P("gx", "gy", "grp"), P("grp", "gx", "gy", None), P("grp", "gx", "gy", None))
    return jax.shard_map(local, mesh=mesh, in_specs=in_specs, out_specs=out_specs, check_vma=False)
```

time: 192 us -> 58.9 us (0.31)
  starting transfers between devices: 142 us -> 0 us
  Pallas kernels: 0 us -> 54.9 us
  other arithmetic: 18 us -> 0 us
  waiting for transfers between devices: 12 us -> 0 us
  between operations: 9.75 us -> 0.65 us
  local copies, waits for them, and re-layouts: 8.78 us -> 3.12 us
    ppermute x34 -> x0, starting transfers between devices: 142 us -> none  [the longest x16 91 us: extended(): lax.ppermute(initial, axis, [(b, a) for a, b in up])]
    pallas_call x0 -> x1, Pallas kernels: none -> 54.9 us  [local(): pl.pallas_call(kernel, out_shape=(jax.ShapeDtypeStruct((8, 16, 128), F32)...]
    ppermute x34 -> x0, waiting for transfers between devices: 12 us -> none  [the longest x16 11.1 us: extended(): lax.ppermute(last, axis, up)]
    scatter-add x8 -> x0, other arithmetic: 10.3 us -> none  [local(): receiver_add = jnp.zeros((total_cells,), jnp.float32).at[flat_cells].add(...]
    add x17 -> x0, other arithmetic: 3.78 us -> none  [the longest x16 3.13 us: laplacian(): accumulated = accumulated + STENCIL[radius] * beside_all]
    concatenate x16 -> x0, other arithmetic: 3.11 us -> none  [extended(): jnp.concatenate([jnp.pad(low, around), shard, jnp.pad(high, around)], axi...]
    slice x27 -> x0, local copies, waits for them, and re-layouts: 3.02 us -> none  [the longest x16 1.11 us: extended(): last = lax.slice_in_dim(shard, length - width, length, axis=dim)]
  transfers between devices with their start and end apart: 34 -> 0, of which waited for: 6 -> 0; matrix products, arithmetic and copies ran while one was open for 9% -> 0% of each run, Pallas kernels for 0% -> 0%
where the time goes in v1:
time: 58.9 us; the launch traced here: 58.7 us
  Pallas kernels  54.9 us (93%)
  local copies, waits for them, and re-layouts  3.12 us (5%)
  between operations  0.65 us (1%)
    pallas_call x1, Pallas kernels, local(): pl.pallas_call(kernel, out_shape=(jax.ShapeDtypeStruct((8, 16, 128), F32)...  54.9 us
    unnamed x7, local copies, waits for them, and re-layouts  3.12 us

profile of v1, /device:TPU:7, one launch (start us, length us, event | category | flops | bytes accessed | tf_op | source)
XLA Modules:
  0.0 58.7 jit_solution(11147525366569633824)
XLA Ops:
  0.6 54.9 %shard_map.103 = (f32[8,16,128]{2,1,0:T(8,128)}, f32[1,8,16,256]{3,2,1,0:T(8,128)}, f32[1,8,16,256]{3,2,1,0:T(8,128)}) custom-call(f32[1,8,16,256]{3,2,1,0:T(8,128)} %now.1, f32[1,8,16,256]{3,2,1,0:T(8,128)} %later.1, f32[8,16,256]{2,1,0:T(8,128)} %courant.1, f32[8,8,128]{2,1,0:T(8,128)} %strips.1, f32[8,1,1,128]{3,2,1,0:T(1,128)} %traces.1, ...), custom_call_target="tpu_custom_call" | custom-call | tf_op jit(solution)/shard_map/pallas_call | solution.py:330
  55.6 0.0 copy-start.1
  55.6 1.5 %copy.14 = f32[8,16,128]{2,1,0:T(8,128)} copy(f32[8,16,128]{2,1,0:T(8,128)} %get-tuple-element.6) | data formatting | bytes 131072
  57.1 0.0 copy-done.1
  57.1 0.0 copy-start
  57.1 0.7 %copy.15 = f32[1,8,16,256]{3,2,1,0:T(8,128)} copy(f32[1,8,16,256]{3,2,1,0:T(8,128)S(1)} %copy-done.1) | data formatting | bytes 262144
  57.8 0.3 copy-done
  58.1 0.7 %copy.16 = f32[1,8,16,256]{3,2,1,0:T(8,128)} copy(f32[1,8,16,256]{3,2,1,0:T(8,128)S(1)} %copy-done) | data formatting | bytes 262144
Async XLA Ops:
  55.6 1.5 %copy-start.1 = (f32[1,8,16,256]{3,2,1,0:T(8,128)S(1)}, f32[1,8,16,256]{3,2,1,0:T(8,128)}, u32[]{:S(2)}) copy-start(f32[1,8,16,256]{3,2,1,0:T(8,128)} %get-tuple-element.7) | copy-start | bytes 393220
  57.1 1.0 %copy-start = (f32[1,8,16,256]{3,2,1,0:T(8,128)S(1)}, f32[1,8,16,256]{3,2,1,0:T(8,128)}, u32[]{:S(2)}) copy-start(f32[1,8,16,256]{3,2,1,0:T(8,128)} %get-tuple-element.8) | copy-start | bytes 393220

commit v2 on v0

v2 whole, which is shorter than its diff:
```python
import jax
import jax.numpy as jnp
from jax import lax
from jax.experimental import pallas as pl
from jax.experimental.pallas import tpu as pltpu
from jax.sharding import PartitionSpec as P

STENCIL = (-205.0 / 72.0, 8.0 / 5.0, -1.0 / 5.0, 8.0 / 315.0, -1.0 / 560.0)
W = (None,) + STENCIL[1:]
MESH = pl.DeviceIdType.MESH
F32 = jnp.float32
BF16 = jnp.bfloat16


def split3(value):
    high = value.astype(BF16).astype(F32)
    rest = value - high
    middle = rest.astype(BF16).astype(F32)
    return high, middle, rest - middle


def shifted_sum(lower, upper, k, lane):
    lower_up, upper_up = pltpu.roll(lower, k, 1), pltpu.roll(upper, k, 1)
    lower_down, upper_down = pltpu.roll(lower, 128 - k, 1), pltpu.roll(upper, 128 - k, 1)
    zero = jnp.zeros_like(lower)
    first, last = lane >= k, lane < 128 - k
    return (
        jnp.where(first, lower_up, zero) + jnp.where(last, lower_down, upper_down),
        jnp.where(first, upper_up, lower_up) + jnp.where(last, upper_down, zero),
    )


def add(total, term):
    return term if total is None else total + term


def kernel(
    now, later, courant, strips, traces, cells, source_in, wavelet_in,
    image_out, now_out, later_out,
    u, t, c, cm, xr, xtr, yr, ytr, cr, xc, yc, xcm, ycm, ys, yts, ycs,
    yl, yh, cl, ch, hx, hy, inj, dense, image_in, image,
    strip_v, trace_v, cell_v, source, wavelet,
    load_sem, xs_sem, xts_sem, ys_sem, yts_sem, cs_sem, xcs_sem, ycs_sem,
    xr_sem, xtr_sem, yr_sem, ytr_sem, cr_sem, xcr_sem, ycr_sem, im_send, im_recv,
):
    group = lax.axis_index("grp")
    at_x = lax.axis_index("gx")
    at_y = lax.axis_index("gy")
    size_x = lax.axis_size("gx")
    size_y = lax.axis_size("gy")
    source_side = group == 0
    has_x = (at_x > 0, at_x < size_x - 1)
    has_y = (at_y > 0, at_y < size_y - 1)
    x_of = (at_x - 1, at_x + 1)
    y_of = (at_y - 1, at_y + 1)
    partner = {"grp": 1 - group}
    corners = [(i, j) for i in range(2) for j in range(2)]
    has_c = {(i, j): jnp.logical_and(has_x[i], has_y[j]) for i, j in corners}

    barrier = pltpu.get_barrier_semaphore()
    count = jnp.int32(1)
    others = [(has_x[d], {"gx": x_of[d]}) for d in range(2)]
    others += [(has_y[d], {"gy": y_of[d]}) for d in range(2)]
    others += [(has_c[i, j], {"gx": x_of[i], "gy": y_of[j]}) for i, j in corners]
    pl.semaphore_signal(barrier, inc=1, device_id=partner, device_id_type=MESH)
    for there, device in others:
        count = count + there.astype(jnp.int32)

        @pl.when(there)
        def _():
            pl.semaphore_signal(barrier, inc=1, device_id=device, device_id_type=MESH)

    loads = []
    for h in range(2):
        zs = pl.ds(128 * h, 128)
        loads.append((now.at[0, :, :, zs], u.at[0, h, :, pl.ds(8, 16)]))
        loads.append((later.at[0, :, :, zs], u.at[1, h, :, pl.ds(8, 16)]))
        loads.append((courant.at[:, :, zs], c.at[h]))
    loads += [(cells, cell_v), (traces, trace_v), (strips, strip_v)]
    loads += [(source_in, source), (wavelet_in, wavelet)]
    loads = [pltpu.make_async_copy(a, b, load_sem.at[i]) for i, (a, b) in enumerate(loads)]
    for copy in loads:
        copy.start()

    for slot in range(2):
        u[slot, :, :, 0:8] = jnp.zeros((2, 8, 8, 128), F32)
        u[slot, :, :, 24:32] = jnp.zeros((2, 8, 8, 128), F32)
    for ref in (yl, yh, cl, ch):
        ref[...] = jnp.zeros_like(ref)
    for d in range(2):

        @pl.when(jnp.logical_not(has_x[d]))
        def _():
            xc[d] = jnp.zeros_like(xc[d])
            for par in range(2):
                xr[par, d] = jnp.zeros_like(xr[par, d])
                xtr[par, d] = jnp.zeros_like(xtr[par, d])

        @pl.when(jnp.logical_not(has_y[d]))
        def _():
            yc[d] = jnp.zeros_like(yc[d])
            for par in range(2):
                yr[par, d] = jnp.zeros_like(yr[par, d])
                ytr[par, d] = jnp.zeros_like(ytr[par, d])

    for i, j in corners:

        @pl.when(jnp.logical_not(has_c[i, j]))
        def _():
            for par in range(2):
                cr[par, i, j] = jnp.zeros_like(cr[par, i, j])

    def remote(src, dst, send, recv, device):
        return pltpu.make_async_remote_copy(
            src_ref=src, dst_ref=dst, send_sem=send, recv_sem=recv,
            device_id=device, device_id_type=MESH,
        )

    def x_copy(par, d):
        return remote(u.at[0, :, pl.ds(4 * d, 4), pl.ds(8, 16)], xr.at[par, 1 - d],
                      xs_sem.at[d], xr_sem.at[par, 1 - d], {"gx": x_of[d]})

    def xt_copy(par, d):
        return remote(t.at[0, :, pl.ds(4 * d, 4)], xtr.at[par, 1 - d],
                      xts_sem.at[d], xtr_sem.at[par, 1 - d], {"gx": x_of[d]})

    def y_copy(par, d):
        return remote(ys.at[d], yr.at[par, 1 - d],
                      ys_sem.at[d], yr_sem.at[par, 1 - d], {"gy": y_of[d]})

    def yt_copy(par, d):
        return remote(yts.at[d], ytr.at[par, 1 - d],
                      yts_sem.at[d], ytr_sem.at[par, 1 - d], {"gy": y_of[d]})

    def corner_copy(par, i, j):
        return remote(ys.at[j, :, pl.ds(4 * i, 4)], cr.at[par, 1 - i, 1 - j],
                      cs_sem.at[i, j], cr_sem.at[par, 1 - i, 1 - j], {"gx": x_of[i], "gy": y_of[j]})

    def xc_copy(d):
        return remote(c.at[:, pl.ds(4 * d, 4)], xc.at[1 - d],
                      xcs_sem.at[d], xcr_sem.at[1 - d], {"gx": x_of[d]})

    def yc_copy(d):
        return remote(ycs.at[d], yc.at[1 - d], ycs_sem.at[d], ycr_sem.at[1 - d], {"gy": y_of[d]})

    def image_copy(slot):
        return remote(u.at[0, 1 - group, :, pl.ds(8, 16)], image_in.at[slot],
                      im_send.at[slot], im_recv.at[slot], partner)

    def start(there, copy):
        @pl.when(there)
        def _():
            copy.start()

    def wait_recv(there, copy):
        @pl.when(there)
        def _():
            copy.wait_recv()

    def wait_send(there, copy):
        @pl.when(there)
        def _():
            copy.wait_send()

    lane = lax.broadcasted_iota(jnp.int32, (16, 128), 1)
    lane4 = lax.broadcasted_iota(jnp.int32, (4, 128), 1)
    lane1 = lax.broadcasted_iota(jnp.int32, (1, 128), 1)
    overwrite = (jnp.logical_and(lane < 4, source_side), jnp.logical_and(lane >= 124, source_side))
    overwrite4 = (jnp.logical_and(lane4 < 4, source_side), jnp.logical_and(lane4 >= 124, source_side))

    for copy in loads:
        copy.wait()

    source_x = source[0] - at_x * 8
    source_y = source[1] - at_y * 16
    inside = (source_x >= 0) & (source_x < 8) & (source_y >= 0) & (source_y < 16)
    source_flat = jnp.where(inside, (source_x * 16 + source_y) * 256 + source[2], -1)
    where_to = jnp.where(source_side, jnp.where(lane1 == 0, source_flat, -1), cell_v[0])
    row_of = jnp.where(where_to < 0, -1, ((where_to >> 7) & 1) * 128 + (where_to >> 8))
    column_of = where_to & 127
    column_hot = jnp.where(
        lax.broadcasted_iota(jnp.int32, (128, 128), 0) == column_of, 1.0, 0.0
    ).astype(BF16)
    row_hot = lax.broadcasted_iota(jnp.int32, (256, 128), 0) == row_of
    layer = lax.broadcasted_iota(jnp.int32, (128, 256), 0) & 7
    depth_of = jnp.where(layer < 4, layer, 248 + layer)
    spread = jnp.where(
        lax.broadcasted_iota(jnp.int32, (128, 256), 1) == depth_of, 1.0, 0.0
    ).astype(BF16)
    own_row = (
        lax.broadcasted_iota(jnp.int32, (8, 16, 128), 2) >> 3
        == lax.broadcasted_iota(jnp.int32, (8, 16, 128), 1)
    )

    def inject(slot, k):
        sample = jnp.where(source_side, jnp.where(lane1 == 0, -wavelet[k], 0.0), trace_v[k, 0])
        total = None
        for part in split3(sample):
            left = jnp.where(row_hot, part, 0.0).astype(BF16)
            total = add(total, lax.dot_general(
                left, column_hot, (((1,), (1,)), ((), ())), preferred_element_type=F32
            ))
        inj[slot] = total.reshape(2, 8, 16, 128)
        total = None
        for part in split3(strip_v[k]):
            left = jnp.where(own_row, part[:, None, :], 0.0).reshape(128, 128).astype(BF16)
            total = add(total, jnp.dot(left, spread, preferred_element_type=F32))
        for h in range(2):
            dense[slot, h] = total[:, 128 * h : 128 * h + 128].reshape(8, 16, 128)

    def own_part(slot, x):
        lower, upper = u[slot, 0, x, 8:24], u[slot, 1, x, 8:24]
        centre = (lower, upper)
        sums = [inj[slot, h, x] + (3.0 * STENCIL[0]) * centre[h] for h in range(2)]
        for k in range(1, 5):
            depth = shifted_sum(lower, upper, k, lane)
            for h in range(2):
                near = depth[h] + (u[slot, h, x, 8 - k : 24 - k] + u[slot, h, x, 8 + k : 24 + k])
                if x - k >= 0:
                    near = near + u[slot, h, x - k, 8:24]
                if x + k < 8:
                    near = near + u[slot, h, x + k, 8:24]
                sums[h] = sums[h] + W[k] * near
        for h in range(2):
            value = 2.0 * centre[h] - u[1 - slot, h, x, 8:24] + cm[h, x] * sums[h]
            value = jnp.where(overwrite[h], dense[slot, h, x], value)
            t[slot, h, x] = value
            if slot == 0:
                yts[0, h, x] = value[0:4]
                yts[1, h, x] = value[12:16]

    def low_rows(ref):
        total = None
        for m in range(4):
            total = add(total, W[4 - m] * ref[m : m + 8])
        return total

    def high_rows(ref):
        total = None
        for m in range(4):
            total = add(total, W[4 - m] * ref[4 - m : 12 - m])
        return total

    def finish(slot, x, planes):
        d = x // 4
        values = []
        for h in range(2):
            extra = None
            for j in range(4):
                distance = x + 4 - j if d == 0 else 8 + j - x
                if distance <= 4:
                    extra = add(extra, W[distance] * planes(h, j))
            low, high = low_rows(yl.at[h, x]), high_rows(yh.at[h, x])
            first = t[slot, h, x, 0:8] + cm[h, x, 0:8] * (extra[0:8] + low)
            second = t[slot, h, x, 8:16] + cm[h, x, 8:16] * (extra[8:16] + high)
            u[1 - slot, h, x, 8:16] = first
            u[1 - slot, h, x, 16:24] = second
            values.append((first, second))
        return values

    def halo(par):
        for i in range(2):
            cl[i, :, :, 0:4] = cr[par, i, 0]
            ch[i, :, :, 8:12] = cr[par, i, 1]
        for d in range(2):
            for h in range(2):
                for j in range(4):
                    extra = None
                    for p in range(8):
                        distance = p + 4 - j if d == 0 else 8 + j - p
                        if distance <= 4:
                            extra = add(extra, W[distance] * u[0, h, p, 8:24])
                    low, high = low_rows(cl.at[d, h, j]), high_rows(ch.at[d, h, j])
                    hx[d, h, j, 0:8] = xcm[d, h, j, 0:8] * (extra[0:8] + low)
                    hx[d, h, j, 8:16] = xcm[d, h, j, 8:16] * (extra[8:16] + high)
        for d in range(2):
            for h in range(2):
                for x in range(8):
                    extra = None
                    for m in range(4):
                        at = 8 - m if d == 0 else 20 + m
                        extra = add(extra, W[4 - m] * u[0, h, x, at : at + 4])
                    i = x // 4
                    for j in range(4):
                        distance = x + 4 - j if i == 0 else 8 + j - x
                        if distance <= 4:
                            extra = extra + W[distance] * cr[par, i, d, h, j]
                    hy[d, h, x] = ycm[d, h, x] * extra

    def send_t(par):
        for d in range(2):
            for x in range(4 * d, 4 * d + 4):
                own_part(0, x)
            if par is not None:
                start(has_x[d], xt_copy(par, d))
        if par is not None:
            for d in range(2):
                start(has_y[d], yt_copy(par, d))

    for h in range(2):
        cm[h] = jnp.where(overwrite[h], 0.0, c[h])
    for d in range(2):
        ys[d] = u[0, :, :, 8 + 12 * d : 12 + 12 * d]
        ycs[d] = c[:, :, 12 * d : 12 * d + 4]
    inject(0, 0)
    send_t(None)

    pl.semaphore_wait(barrier, count)
    for d in range(2):
        start(has_x[d], x_copy(0, d))
    for d in range(2):
        start(has_y[d], y_copy(0, d))
    for i, j in corners:
        start(has_c[i, j], corner_copy(0, i, j))
    for d in range(2):
        start(has_x[d], xc_copy(d))
    for d in range(2):
        start(has_y[d], yc_copy(d))
    for d in range(2):
        start(has_x[d], xt_copy(0, d))
    for d in range(2):
        start(has_y[d], yt_copy(0, d))

    def one_round(half, par):
        first, final = half == 0, half == 1
        more = True if par == 0 else first
        step = 4 * half + 2 * par
        inject(1, step + 1)
        if par == 0:
            inject(0, step + 2)

            @pl.when(final)
            def _():
                image_copy(0).wait()
                image[...] = u[0, group, :, 8:24] * image_in[0]

        else:

            @pl.when(more)
            def _():
                inject(0, step + 2)

        for d in range(2):
            wait_recv(has_y[d], y_copy(par, 1 - d))
        for x in range(8):
            yl[:, x, 0:4] = yr[par, 0, :, x]
            yh[:, x, 8:12] = yr[par, 1, :, x]
        for d in range(2):
            wait_recv(has_x[d], x_copy(par, 1 - d))
            for x in range(4 * d, 4 * d + 4):
                finish(0, x, lambda h, j: xr[par, d, h, j])

        for x in range(8):
            own_part(1, x)
        if par == 0:

            @pl.when(first)
            def _():
                for d in range(2):
                    wait_recv(has_x[d], xc_copy(1 - d))
                    wait_recv(has_y[d], yc_copy(1 - d))
                    for h in range(2):
                        xcm[d, h] = jnp.where(overwrite[h], 0.0, xc[d, h])
                        ycm[d, h] = jnp.where(overwrite4[h], 0.0, yc[d, h])
                for d in range(2):
                    wait_send(has_x[d], xc_copy(d))
                    wait_send(has_y[d], yc_copy(d))

        else:

            @pl.when(final)
            def _():
                for h in range(2):
                    later_out[0, :, :, 128 * h : 128 * h + 128] = u[1, h, :, 8:24]

        for i, j in corners:
            wait_recv(has_c[i, j], corner_copy(par, 1 - i, 1 - j))
        halo(par)
        for d in range(2):
            wait_send(has_x[d], x_copy(par, d))
            wait_send(has_y[d], y_copy(par, d))
        for i, j in corners:
            wait_send(has_c[i, j], corner_copy(par, i, j))
        for d in range(2):
            wait_recv(has_y[d], yt_copy(par, 1 - d))
        for x in range(8):
            for h in range(2):
                yl[h, x, 0:4] = ytr[par, 0, h, x] + hy[0, h, x]
                yh[h, x, 8:12] = ytr[par, 1, h, x] + hy[1, h, x]
        for d in range(2):
            wait_recv(has_x[d], xt_copy(par, 1 - d))
            for h in range(2):
                for j in range(4):
                    hx[d, h, j] = hx[d, h, j] + xtr[par, d, h, j]
            for x in range(4 * d, 4 * d + 4):
                values = finish(1, x, lambda h, j: hx[d, h, j])
                for h in range(2):
                    ys[0, h, x] = values[h][0][0:4]
                    ys[1, h, x] = values[h][1][4:8]
            start(jnp.logical_and(more, has_x[d]), x_copy(1 - par, d))
        for d in range(2):
            start(jnp.logical_and(more, has_y[d]), y_copy(1 - par, d))
        for i, j in corners:
            start(jnp.logical_and(more, has_c[i, j]), corner_copy(1 - par, i, j))
        for d in range(2):
            wait_send(has_x[d], xt_copy(par, d))
            wait_send(has_y[d], yt_copy(par, d))
        if par == 0:
            send_t(1 - par)
        else:

            @pl.when(first)
            def _():
                image_copy(0).start()
                send_t(1 - par)

            @pl.when(final)
            def _():
                image_copy(1).start()

    def two_rounds(half, carry):
        one_round(half, 0)
        one_round(half, 1)
        return carry

    lax.fori_loop(0, 2, two_rounds, 0)
    for h in range(2):
        now_out[0, :, :, 128 * h : 128 * h + 128] = u[0, h, :, 8:24]
    image_copy(1).wait()
    image_out[...] = image[...] + u[0, group, :, 8:24] * image_in[1]


def local(state_now, state_later, courant, strips, traces, receiver_cells, source_point, wavelet):
    any_space = pl.BlockSpec(memory_space=pl.ANY)
    vmem = pl.BlockSpec(memory_space=pltpu.VMEM)
    dma = pltpu.SemaphoreType.DMA
    v = pltpu.VMEM
    return pl.pallas_call(
        kernel,
        out_shape=(
            jax.ShapeDtypeStruct((8, 16, 128), F32),
            jax.ShapeDtypeStruct((1, 8, 16, 256), F32),
            jax.ShapeDtypeStruct((1, 8, 16, 256), F32),
        ),
        in_specs=[any_space] * 8,
        out_specs=(vmem,) * 3,
        scratch_shapes=[
            v((2, 2, 8, 32, 128), F32),
            v((2, 2, 8, 16, 128), F32),
            v((2, 8, 16, 128), F32),
            v((2, 8, 16, 128), F32),
            v((2, 2, 2, 4, 16, 128), F32),
            v((2, 2, 2, 4, 16, 128), F32),
            v((2, 2, 2, 8, 4, 128), F32),
            v((2, 2, 2, 8, 4, 128), F32),
            v((2, 2, 2, 2, 4, 4, 128), F32),
            v((2, 2, 4, 16, 128), F32),
            v((2, 2, 8, 4, 128), F32),
            v((2, 2, 4, 16, 128), F32),
            v((2, 2, 8, 4, 128), F32),
            v((2, 2, 8, 4, 128), F32),
            v((2, 2, 8, 4, 128), F32),
            v((2, 2, 8, 4, 128), F32),
            v((2, 8, 16, 128), F32),
            v((2, 8, 16, 128), F32),
            v((2, 2, 4, 16, 128), F32),
            v((2, 2, 4, 16, 128), F32),
            v((2, 2, 4, 16, 128), F32),
            v((2, 2, 8, 4, 128), F32),
            v((2, 2, 8, 16, 128), F32),
            v((2, 2, 8, 16, 128), F32),
            v((2, 8, 16, 128), F32),
            v((8, 16, 128), F32),
            v((8, 8, 128), F32),
            v((8, 1, 1, 128), F32),
            v((1, 1, 128), jnp.int32),
            pltpu.SMEM((3,), jnp.int32),
            pltpu.SMEM((8,), F32),
            dma((11,)),
            dma((2,)), dma((2,)), dma((2,)), dma((2,)), dma((2, 2)), dma((2,)), dma((2,)),
            dma((2, 2)), dma((2, 2)), dma((2, 2)), dma((2, 2)), dma((2, 2, 2)), dma((2,)), dma((2,)),
            dma((2,)), dma((2,)),
        ],
        compiler_params=pltpu.CompilerParams(collective_id=0, has_side_effects=True),
    )(state_now, state_later, courant, strips, traces, receiver_cells, source_point, wavelet)


def solution(mesh):
    in_specs = (
        P("grp", "gx", "gy", None),
        P("grp", "gx", "gy", None),
        P("gx", "gy", None),
        P(None, "gx", "gy"),
        P(None, "gx", "gy", None),
        P("gx", "gy", None),
        P(),
        P(),
    )
    out_specs = (P("gx", "gy", "grp"), P("grp", "gx", "gy", None), P("grp", "gx", "gy", None))
    return jax.shard_map(local, mesh=mesh, in_specs=in_specs, out_specs=out_specs, check_vma=False)
```

time: 192 us -> 47.1 us (0.25)
  starting transfers between devices: 142 us -> 0 us
  Pallas kernels: 0 us -> 43.1 us
  other arithmetic: 18 us -> 0 us
  waiting for transfers between devices: 12 us -> 0 us
  between operations: 9.75 us -> 0.65 us
  local copies, waits for them, and re-layouts: 8.78 us -> 3.12 us
    ppermute x34 -> x0, starting transfers between devices: 142 us -> none  [the longest x16 91 us: extended(): lax.ppermute(initial, axis, [(b, a) for a, b in up])]
    pallas_call x0 -> x1, Pallas kernels: none -> 43.1 us  [local(): pl.pallas_call(kernel, out_shape=(jax.ShapeDtypeStruct((8, 16, 128), F32)...]
    ppermute x34 -> x0, waiting for transfers between devices: 12 us -> none  [the longest x16 11.1 us: extended(): lax.ppermute(last, axis, up)]
    scatter-add x8 -> x0, other arithmetic: 10.3 us -> none  [local(): receiver_add = jnp.zeros((total_cells,), jnp.float32).at[flat_cells].add(...]
    add x17 -> x0, other arithmetic: 3.78 us -> none  [the longest x16 3.13 us: laplacian(): accumulated = accumulated + STENCIL[radius] * beside_all]
    concatenate x16 -> x0, other arithmetic: 3.11 us -> none  [extended(): jnp.concatenate([jnp.pad(low, around), shard, jnp.pad(high, around)], axi...]
    slice x27 -> x0, local copies, waits for them, and re-layouts: 3.02 us -> none  [the longest x16 1.11 us: extended(): last = lax.slice_in_dim(shard, length - width, length, axis=dim)]
  transfers between devices with their start and end apart: 34 -> 0, of which waited for: 6 -> 0; matrix products, arithmetic and copies ran while one was open for 9% -> 0% of each run, Pallas kernels for 0% -> 0%
where the time goes in v2:
time: 47.1 us; the launch traced here: 46.9 us
  Pallas kernels  43.1 us (92%)
  local copies, waits for them, and re-layouts  3.12 us (7%)
  between operations  0.65 us (1%)
    pallas_call x1, Pallas kernels, local(): pl.pallas_call(kernel, out_shape=(jax.ShapeDtypeStruct((8, 16, 128), F32)...  43.1 us
    unnamed x7, local copies, waits for them, and re-layouts  3.12 us

profile of v2, /device:TPU:7, one launch (start us, length us, event | category | flops | bytes accessed | tf_op | source)
XLA Modules:
  0.0 46.9 jit_solution(9256602950260447236)
XLA Ops:
  0.6 43.1 %shard_map.103 = (f32[8,16,128]{2,1,0:T(8,128)}, f32[1,8,16,256]{3,2,1,0:T(8,128)}, f32[1,8,16,256]{3,2,1,0:T(8,128)}) custom-call(f32[1,8,16,256]{3,2,1,0:T(8,128)} %now.1, f32[1,8,16,256]{3,2,1,0:T(8,128)} %later.1, f32[8,16,256]{2,1,0:T(8,128)} %courant.1, f32[8,8,128]{2,1,0:T(8,128)} %strips.1, f32[8,1,1,128]{3,2,1,0:T(1,128)} %traces.1, ...), custom_call_target="tpu_custom_call" | custom-call | tf_op jit(solution)/shard_map/pallas_call | solution.py:438
  43.7 0.0 copy-start.1
  43.7 1.5 %copy.14 = f32[8,16,128]{2,1,0:T(8,128)} copy(f32[8,16,128]{2,1,0:T(8,128)} %get-tuple-element.6) | data formatting | bytes 131072
  45.3 0.0 copy-done.1
  45.3 0.0 copy-start
  45.3 0.7 %copy.15 = f32[1,8,16,256]{3,2,1,0:T(8,128)} copy(f32[1,8,16,256]{3,2,1,0:T(8,128)S(1)} %copy-done.1) | data formatting | bytes 262144
  45.9 0.3 copy-done
  46.2 0.7 %copy.16 = f32[1,8,16,256]{3,2,1,0:T(8,128)} copy(f32[1,8,16,256]{3,2,1,0:T(8,128)S(1)} %copy-done) | data formatting | bytes 262144
Async XLA Ops:
  43.7 1.5 %copy-start.1 = (f32[1,8,16,256]{3,2,1,0:T(8,128)S(1)}, f32[1,8,16,256]{3,2,1,0:T(8,128)}, u32[]{:S(2)}) copy-start(f32[1,8,16,256]{3,2,1,0:T(8,128)} %get-tuple-element.7) | copy-start | bytes 393220
  45.3 1.0 %copy-start = (f32[1,8,16,256]{3,2,1,0:T(8,128)S(1)}, f32[1,8,16,256]{3,2,1,0:T(8,128)}, u32[]{:S(2)}) copy-start(f32[1,8,16,256]{3,2,1,0:T(8,128)} %get-tuple-element.8) | copy-start | bytes 393220

commit v3 on v2

--- a/solution.py
+++ b/solution.py
@@ -41,7 +41,7 @@
     yl, yh, cl, ch, hx, hy, inj, dense, image_in, image,
     strip_v, trace_v, cell_v, source, wavelet,
     load_sem, xs_sem, xts_sem, ys_sem, yts_sem, cs_sem, xcs_sem, ycs_sem,
-    xr_sem, xtr_sem, yr_sem, ytr_sem, cr_sem, xcr_sem, ycr_sem, im_send, im_recv,
+    xr_sem, xtr_sem, yr_sem, ytr_sem, cr_sem, xcr_sem, ycr_sem, im_send, im_recv, ready,
 ):
     group = lax.axis_index("grp")
     at_x = lax.axis_index("gx")
@@ -61,7 +61,6 @@
     count = jnp.int32(1)
     others = [(has_x[d], {"gx": x_of[d]}) for d in range(2)]
     others += [(has_y[d], {"gy": y_of[d]}) for d in range(2)]
-    others += [(has_c[i, j], {"gx": x_of[i], "gy": y_of[j]}) for i, j in corners]
     pl.semaphore_signal(barrier, inc=1, device_id=partner, device_id_type=MESH)
     for there, device in others:
         count = count + there.astype(jnp.int32)
@@ -258,10 +257,7 @@
             values.append((first, second))
         return values
 
-    def halo(par):
-        for i in range(2):
-            cl[i, :, :, 0:4] = cr[par, i, 0]
-            ch[i, :, :, 8:12] = cr[par, i, 1]
+    def halo_cross():
         for d in range(2):
             for h in range(2):
                 for j in range(4):
@@ -270,22 +266,34 @@
                         distance = p + 4 - j if d == 0 else 8 + j - p
                         if distance <= 4:
                             extra = add(extra, W[distance] * u[0, h, p, 8:24])
-                    low, high = low_rows(cl.at[d, h, j]), high_rows(ch.at[d, h, j])
-                    hx[d, h, j, 0:8] = xcm[d, h, j, 0:8] * (extra[0:8] + low)
-                    hx[d, h, j, 8:16] = xcm[d, h, j, 8:16] * (extra[8:16] + high)
-        for d in range(2):
-            for h in range(2):
+                    hx[d, h, j] = extra
                 for x in range(8):
                     extra = None
                     for m in range(4):
                         at = 8 - m if d == 0 else 20 + m
                         extra = add(extra, W[4 - m] * u[0, h, x, at : at + 4])
-                    i = x // 4
+                    hy[d, h, x] = extra
+
+    def halo_corners(par, i):
+        cl[i, :, :, 0:4] = cr[par, i, 0]
+        ch[i, :, :, 8:12] = cr[par, i, 1]
+        for h in range(2):
+            for j in range(4):
+                low, high = low_rows(cl.at[i, h, j]), high_rows(ch.at[i, h, j])
+                for rows, extra in ((slice(0, 8), low), (slice(8, 16), high)):
+                    hx[i, h, j, rows] = xtr[par, i, h, j, rows] + xcm[i, h, j, rows] * (hx[i, h, j, rows] + extra)
+            for x in range(4 * i, 4 * i + 4):
+                for d in range(2):
+                    extra = hy[d, h, x]
                     for j in range(4):
                         distance = x + 4 - j if i == 0 else 8 + j - x
                         if distance <= 4:
                             extra = extra + W[distance] * cr[par, i, d, h, j]
-                    hy[d, h, x] = ycm[d, h, x] * extra
+                    value = ytr[par, d, h, x] + ycm[d, h, x] * extra
+                    if d == 0:
+                        yl[h, x, 0:4] = value
+                    else:
+                        yh[h, x, 8:12] = value
 
     def send_t(par):
         for d in range(2):
@@ -310,16 +318,28 @@
         start(has_x[d], x_copy(0, d))
     for d in range(2):
         start(has_y[d], y_copy(0, d))
-    for i, j in corners:
-        start(has_c[i, j], corner_copy(0, i, j))
+    for d in range(2):
+
+        @pl.when(has_y[d])
+        def _():
+            pl.semaphore_signal(ready.at[1 - d], inc=1, device_id={"gy": y_of[d]}, device_id_type=MESH)
+
+    for d in range(2):
+        start(has_x[d], xt_copy(0, d))
+    for d in range(2):
+        start(has_y[d], yt_copy(0, d))
+    for j in range(2):
+
+        @pl.when(has_y[j])
+        def _():
+            pl.semaphore_wait(ready.at[j], 1)
+
+        for i in range(2):
+            start(has_c[i, j], corner_copy(0, i, j))
     for d in range(2):
         start(has_x[d], xc_copy(d))
     for d in range(2):
         start(has_y[d], yc_copy(d))
-    for d in range(2):
-        start(has_x[d], xt_copy(0, d))
-    for d in range(2):
-        start(has_y[d], yt_copy(0, d))
 
     def one_round(half, par):
         first, final = half == 0, half == 1
@@ -352,6 +372,7 @@
 
         for x in range(8):
             own_part(1, x)
+        halo_cross()
         if par == 0:
 
             @pl.when(first)
@@ -373,9 +394,6 @@
                 for h in range(2):
                     later_out[0, :, :, 128 * h : 128 * h + 128] = u[1, h, :, 8:24]
 
-        for i, j in corners:
-            wait_recv(has_c[i, j], corner_copy(par, 1 - i, 1 - j))
-        halo(par)
         for d in range(2):
             wait_send(has_x[d], x_copy(par, d))
             wait_send(has_y[d], y_copy(par, d))
@@ -383,25 +401,21 @@
             wait_send(has_c[i, j], corner_copy(par, i, j))
         for d in range(2):
             wait_recv(has_y[d], yt_copy(par, 1 - d))
-        for x in range(8):
-            for h in range(2):
-                yl[h, x, 0:4] = ytr[par, 0, h, x] + hy[0, h, x]
-                yh[h, x, 8:12] = ytr[par, 1, h, x] + hy[1, h, x]
-        for d in range(2):
+        for d in range(2):
+            for j in range(2):
+                wait_recv(has_c[d, j], corner_copy(par, 1 - d, 1 - j))
             wait_recv(has_x[d], xt_copy(par, 1 - d))
-            for h in range(2):
-                for j in range(4):
-                    hx[d, h, j] = hx[d, h, j] + xtr[par, d, h, j]
+            halo_corners(par, d)
             for x in range(4 * d, 4 * d + 4):
                 values = finish(1, x, lambda h, j: hx[d, h, j])
                 for h in range(2):
                     ys[0, h, x] = values[h][0][0:4]
                     ys[1, h, x] = values[h][1][4:8]
+            for j in range(2):
+                start(jnp.logical_and(more, has_c[d, j]), corner_copy(1 - par, d, j))
             start(jnp.logical_and(more, has_x[d]), x_copy(1 - par, d))
         for d in range(2):
             start(jnp.logical_and(more, has_y[d]), y_copy(1 - par, d))
-        for i, j in corners:
-            start(jnp.logical_and(more, has_c[i, j]), corner_copy(1 - par, i, j))
         for d in range(2):
             wait_send(has_x[d], xt_copy(par, d))
             wait_send(has_y[d], yt_copy(par, d))
@@ -438,9 +452,9 @@
     return pl.pallas_call(
         kernel,
         out_shape=(
-            jax.ShapeDtypeStruct((8, 16, 128), F32),
-            jax.ShapeDtypeStruct((1, 8, 16, 256), F32),
-            jax.ShapeDtypeStruct((1, 8, 16, 256), F32),
+            v((8, 16, 128), F32),
+            v((1, 8, 16, 256), F32),
+            v((1, 8, 16, 256), F32),
         ),
         in_specs=[any_space] * 8,
         out_specs=(vmem,) * 3,
@@ -480,6 +494,7 @@
             dma((2,)), dma((2,)), dma((2,)), dma((2,)), dma((2, 2)), dma((2,)), dma((2,)),
             dma((2, 2)), dma((2, 2)), dma((2, 2)), dma((2, 2)), dma((2, 2, 2)), dma((2,)), dma((2,)),
             dma((2,)), dma((2,)),
+            pltpu.SemaphoreType.REGULAR((2,)),
         ],
         compiler_params=pltpu.CompilerParams(collective_id=0, has_side_effects=True),
     )(state_now, state_later, courant, strips, traces, receiver_cells, source_point, wavelet)

time: 47.1 us -> 43.7 us (0.928)
  Pallas kernels: 43.1 us -> 41 us
  local copies, waits for them, and re-layouts: 3.12 us -> 1.94 us
    pallas_call x1, Pallas kernels: 43.1 us -> 41 us  [local(): pl.pallas_call(kernel, out_shape=(v((8, 16, 128), F32), v((1, 8, 16, 256)...]
    unnamed x7 -> x3, local copies, waits for them, and re-layouts: 3.12 us -> 1.94 us
where the time goes in v3:
time: 43.7 us; the launch traced here: 43.5 us
  Pallas kernels  41 us (94%)
  local copies, waits for them, and re-layouts  1.94 us (4%)
  between operations  0.64 us (1%)
    pallas_call x1, Pallas kernels, local(): pl.pallas_call(kernel, out_shape=(v((8, 16, 128), F32), v((1, 8, 16, 256)...  41 us
    unnamed x3, local copies, waits for them, and re-layouts  1.94 us

profile of v3, /device:TPU:7, one launch (start us, length us, event | category | flops | bytes accessed | tf_op | source)
XLA Modules:
  0.0 43.5 jit_solution(2236954932591593545)
XLA Ops:
  0.6 41.0 %shard_map.103 = (f32[8,16,128]{2,1,0:T(8,128)S(1)}, f32[1,8,16,256]{3,2,1,0:T(8,128)S(1)}, f32[1,8,16,256]{3,2,1,0:T(8,128)S(1)}) custom-call(f32[1,8,16,256]{3,2,1,0:T(8,128)} %now.1, f32[1,8,16,256]{3,2,1,0:T(8,128)} %later.1, f32[8,16,256]{2,1,0:T(8,128)} %courant.1, f32[8,8,128]{2,1,0:T(8,128)} %strips.1, f32[8,1,1,128]{3,2,1,0:T(1,128)} %traces.1, ...), custom_call_target="tpu_custom_call" | custom-call | tf_op jit(solution)/shard_map/pallas_call | solution.py:452
  41.6 0.6 %copy.14 = f32[8,16,128]{2,1,0:T(8,128)} copy(f32[8,16,128]{2,1,0:T(8,128)S(1)} %get-tuple-element.3) | data formatting | bytes 131072
  42.2 0.7 %copy.15 = f32[1,8,16,256]{3,2,1,0:T(8,128)} copy(f32[1,8,16,256]{3,2,1,0:T(8,128)S(1)} %get-tuple-element.4) | data formatting | bytes 262144
  42.9 0.7 %copy.16 = f32[1,8,16,256]{3,2,1,0:T(8,128)} copy(f32[1,8,16,256]{3,2,1,0:T(8,128)S(1)} %get-tuple-element.5) | data formatting | bytes 262144

commit v4 on v3

--- a/solution.py
+++ b/solution.py
@@ -81,6 +81,80 @@
     for copy in loads:
         copy.start()
 
+    def remote(src, dst, send, recv, device):
+        return pltpu.make_async_remote_copy(
+            src_ref=src, dst_ref=dst, send_sem=send, recv_sem=recv,
+            device_id=device, device_id_type=MESH,
+        )
+
+    def x_copy(par, d):
+        return remote(u.at[0, :, pl.ds(4 * d, 4), pl.ds(8, 16)], xr.at[par, 1 - d],
+                      xs_sem.at[d], xr_sem.at[par, 1 - d], {"gx": x_of[d]})
+
+    def xt_copy(par, d):
+        return remote(t.at[0, :, pl.ds(4 * d, 4)], xtr.at[par, 1 - d],
+                      xts_sem.at[d], xtr_sem.at[par, 1 - d], {"gx": x_of[d]})
+
+    def y_copy(par, d):
+        return remote(ys.at[d], yr.at[par, 1 - d],
+                      ys_sem.at[d], yr_sem.at[par, 1 - d], {"gy": y_of[d]})
+
+    def yt_copy(par, d):
+        return remote(yts.at[d], ytr.at[par, 1 - d],
+                      yts_sem.at[d], ytr_sem.at[par, 1 - d], {"gy": y_of[d]})
+
+    def corner_copy(par, i, j):
+        return remote(ys.at[j, :, pl.ds(4 * i, 4)], cr.at[par, 1 - i, 1 - j],
+                      cs_sem.at[i, j], cr_sem.at[par, 1 - i, 1 - j], {"gx": x_of[i], "gy": y_of[j]})
+
+    def xc_copy(d):
+        return remote(c.at[:, pl.ds(4 * d, 4)], xc.at[1 - d],
+                      xcs_sem.at[d], xcr_sem.at[1 - d], {"gx": x_of[d]})
+
+    def x_first(d, h):
+        return remote(now.at[0, pl.ds(4 * d, 4), :, pl.ds(128 * h, 128)], xr.at[0, 1 - d, h],
+                      xs_sem.at[d], xr_sem.at[0, 1 - d], {"gx": x_of[d]})
+
+    def xc_first(d, h):
+        return remote(courant.at[pl.ds(4 * d, 4), :, pl.ds(128 * h, 128)], xc.at[1 - d, h],
+                      xcs_sem.at[d], xcr_sem.at[1 - d], {"gx": x_of[d]})
+
+    def yc_copy(d):
+        return remote(ycs.at[d], yc.at[1 - d], ycs_sem.at[d], ycr_sem.at[1 - d], {"gy": y_of[d]})
+
+    def image_copy(slot):
+        return remote(u.at[0, 1 - group, :, pl.ds(8, 16)], image_in.at[slot],
+                      im_send.at[slot], im_recv.at[slot], partner)
+
+    def start(there, copy):
+        @pl.when(there)
+        def _():
+            copy.start()
+
+    def wait_recv(there, copy):
+        @pl.when(there)
+        def _():
+            copy.wait_recv()
+
+    def wait_send(there, copy):
+        @pl.when(there)
+        def _():
+            copy.wait_send()
+
+    pl.semaphore_wait(barrier, count)
+    for d in range(2):
+        for h in range(2):
+            start(has_x[d], x_first(d, h))
+    for d in range(2):
+
+        @pl.when(has_y[d])
+        def _():
+            pl.semaphore_signal(ready.at[1 - d], inc=1, device_id={"gy": y_of[d]}, device_id_type=MESH)
+
+    for d in range(2):
+        for h in range(2):
+            start(has_x[d], xc_first(d, h))
+
     for slot in range(2):
         u[slot, :, :, 0:8] = jnp.zeros((2, 8, 8, 128), F32)
         u[slot, :, :, 24:32] = jnp.zeros((2, 8, 8, 128), F32)
@@ -109,66 +183,27 @@
             for par in range(2):
                 cr[par, i, j] = jnp.zeros_like(cr[par, i, j])
 
-    def remote(src, dst, send, recv, device):
-        return pltpu.make_async_remote_copy(
-            src_ref=src, dst_ref=dst, send_sem=send, recv_sem=recv,
-            device_id=device, device_id_type=MESH,
-        )
-
-    def x_copy(par, d):
-        return remote(u.at[0, :, pl.ds(4 * d, 4), pl.ds(8, 16)], xr.at[par, 1 - d],
-                      xs_sem.at[d], xr_sem.at[par, 1 - d], {"gx": x_of[d]})
-
-    def xt_copy(par, d):
-        return remote(t.at[0, :, pl.ds(4 * d, 4)], xtr.at[par, 1 - d],
-                      xts_sem.at[d], xtr_sem.at[par, 1 - d], {"gx": x_of[d]})
-
-    def y_copy(par, d):
-        return remote(ys.at[d], yr.at[par, 1 - d],
-                      ys_sem.at[d], yr_sem.at[par, 1 - d], {"gy": y_of[d]})
-
-    def yt_copy(par, d):
-        return remote(yts.at[d], ytr.at[par, 1 - d],
-                      yts_sem.at[d], ytr_sem.at[par, 1 - d], {"gy": y_of[d]})
-
-    def corner_copy(par, i, j):
-        return remote(ys.at[j, :, pl.ds(4 * i, 4)], cr.at[par, 1 - i, 1 - j],
-                      cs_sem.at[i, j], cr_sem.at[par, 1 - i, 1 - j], {"gx": x_of[i], "gy": y_of[j]})
-
-    def xc_copy(d):
-        return remote(c.at[:, pl.ds(4 * d, 4)], xc.at[1 - d],
-                      xcs_sem.at[d], xcr_sem.at[1 - d], {"gx": x_of[d]})
-
-    def yc_copy(d):
-        return remote(ycs.at[d], yc.at[1 - d], ycs_sem.at[d], ycr_sem.at[1 - d], {"gy": y_of[d]})
-
-    def image_copy(slot):
-        return remote(u.at[0, 1 - group, :, pl.ds(8, 16)], image_in.at[slot],
-                      im_send.at[slot], im_recv.at[slot], partner)
-
-    def start(there, copy):
-        @pl.when(there)
-        def _():
-            copy.start()
-
-    def wait_recv(there, copy):
-        @pl.when(there)
-        def _():
-            copy.wait_recv()
-
-    def wait_send(there, copy):
-        @pl.when(there)
-        def _():
-            copy.wait_send()
-
     lane = lax.broadcasted_iota(jnp.int32, (16, 128), 1)
     lane4 = lax.broadcasted_iota(jnp.int32, (4, 128), 1)
     lane1 = lax.broadcasted_iota(jnp.int32, (1, 128), 1)
     overwrite = (jnp.logical_and(lane < 4, source_side), jnp.logical_and(lane >= 124, source_side))
     overwrite4 = (jnp.logical_and(lane4 < 4, source_side), jnp.logical_and(lane4 >= 124, source_side))
 
-    for copy in loads:
-        copy.wait()
+    for i in (0, 3):
+        loads[i].wait()
+    for d in range(2):
+        ys[d] = u[0, :, :, 8 + 12 * d : 12 + 12 * d]
+        start(has_y[d], y_copy(0, d))
+    for j in range(2):
+
+        @pl.when(has_y[j])
+        def _():
+            pl.semaphore_wait(ready.at[j], 1)
+
+        for i in range(2):
+            start(has_c[i, j], corner_copy(0, i, j))
+    for i in (1, 2, 4, 5, 6, 7, 8, 9, 10):
+        loads[i].wait()
 
     source_x = source[0] - at_x * 8
     source_y = source[1] - at_y * 16
@@ -281,7 +316,7 @@
             for j in range(4):
                 low, high = low_rows(cl.at[i, h, j]), high_rows(ch.at[i, h, j])
                 for rows, extra in ((slice(0, 8), low), (slice(8, 16), high)):
-                    hx[i, h, j, rows] = xtr[par, i, h, j, rows] + xcm[i, h, j, rows] * (hx[i, h, j, rows] + extra)
+                    hx[i, h, j, rows] = xcm[i, h, j, rows] * (hx[i, h, j, rows] + extra)
             for x in range(4 * i, 4 * i + 4):
                 for d in range(2):
                     extra = hy[d, h, x]
@@ -299,46 +334,16 @@
         for d in range(2):
             for x in range(4 * d, 4 * d + 4):
                 own_part(0, x)
-            if par is not None:
-                start(has_x[d], xt_copy(par, d))
-        if par is not None:
-            for d in range(2):
-                start(has_y[d], yt_copy(par, d))
+            start(has_x[d], xt_copy(par, d))
+        for d in range(2):
+            start(has_y[d], yt_copy(par, d))
 
     for h in range(2):
         cm[h] = jnp.where(overwrite[h], 0.0, c[h])
+    inject(0, 0)
+    send_t(0)
     for d in range(2):
-        ys[d] = u[0, :, :, 8 + 12 * d : 12 + 12 * d]
         ycs[d] = c[:, :, 12 * d : 12 * d + 4]
-    inject(0, 0)
-    send_t(None)
-
-    pl.semaphore_wait(barrier, count)
-    for d in range(2):
-        start(has_x[d], x_copy(0, d))
-    for d in range(2):
-        start(has_y[d], y_copy(0, d))
-    for d in range(2):
-
-        @pl.when(has_y[d])
-        def _():
-            pl.semaphore_signal(ready.at[1 - d], inc=1, device_id={"gy": y_of[d]}, device_id_type=MESH)
-
-    for d in range(2):
-        start(has_x[d], xt_copy(0, d))
-    for d in range(2):
-        start(has_y[d], yt_copy(0, d))
-    for j in range(2):
-
-        @pl.when(has_y[j])
-        def _():
-            pl.semaphore_wait(ready.at[j], 1)
-
-        for i in range(2):
-            start(has_c[i, j], corner_copy(0, i, j))
-    for d in range(2):
-        start(has_x[d], xc_copy(d))
-    for d in range(2):
         start(has_y[d], yc_copy(d))
 
     def one_round(half, par):
@@ -404,10 +409,10 @@
         for d in range(2):
             for j in range(2):
                 wait_recv(has_c[d, j], corner_copy(par, 1 - d, 1 - j))
+            halo_corners(par, d)
             wait_recv(has_x[d], xt_copy(par, 1 - d))
-            halo_corners(par, d)
             for x in range(4 * d, 4 * d + 4):
-                values = finish(1, x, lambda h, j: hx[d, h, j])
+                values = finish(1, x, lambda h, j: xtr[par, d, h, j] + hx[d, h, j])
                 for h in range(2):
                     ys[0, h, x] = values[h][0][0:4]
                     ys[1, h, x] = values[h][1][4:8]
@@ -444,12 +449,21 @@
     image_out[...] = image[...] + u[0, group, :, 8:24] * image_in[1]
 
 
+def hand_out(image_in, now_in, later_in, image_out, now_out, later_out, sem):
+    pairs = ((now_in, now_out), (later_in, later_out), (image_in, image_out))
+    copies = [pltpu.make_async_copy(a, b, sem.at[i]) for i, (a, b) in enumerate(pairs)]
+    for copy in copies:
+        copy.start()
+    for copy in copies:
+        copy.wait()
+
+
 def local(state_now, state_later, courant, strips, traces, receiver_cells, source_point, wavelet):
     any_space = pl.BlockSpec(memory_space=pl.ANY)
     vmem = pl.BlockSpec(memory_space=pltpu.VMEM)
     dma = pltpu.SemaphoreType.DMA
     v = pltpu.VMEM
-    return pl.pallas_call(
+    results = pl.pallas_call(
         kernel,
         out_shape=(
             v((8, 16, 128), F32),
@@ -498,6 +512,13 @@
         ],
         compiler_params=pltpu.CompilerParams(collective_id=0, has_side_effects=True),
     )(state_now, state_later, courant, strips, traces, receiver_cells, source_point, wavelet)
+    return pl.pallas_call(
+        hand_out,
+        out_shape=tuple(jax.ShapeDtypeStruct(r.shape, F32) for r in results),
+        in_specs=[vmem] * 3,
+        out_specs=(any_space,) * 3,
+        scratch_shapes=[dma((3,))],
+    )(*[pltpu.with_memory_space_constraint(r, pltpu.VMEM) for r in results])
 
 
 def solution(mesh):

time: 43.7 us -> 42.6 us (0.975)
  local copies, waits for them, and re-layouts: 1.94 us -> 0 us
  Pallas kernels: 41 us -> 41.8 us
    unnamed x3 -> x0, local copies, waits for them, and re-layouts: 1.94 us -> none
    pallas_call x0 -> x1, Pallas kernels: none -> 0.74 us  [local(): pl.pallas_call(hand_out, out_shape=tuple((jax.ShapeDtypeStruct(r.shape, F...]
where the time goes in v4:
time: 42.6 us; the launch traced here: 42.4 us
  Pallas kernels  41.8 us (98%)
  between operations  0.64 us (2%)
    pallas_call x1, Pallas kernels, local(): pl.pallas_call(kernel, out_shape=(v((8, 16, 128), F32), v((1, 8, 16, 256)...  41 us

profile of v4, /device:TPU:7, one launch (start us, length us, event | category | flops | bytes accessed | tf_op | source)
XLA Modules:
  0.0 42.4 jit_solution(4456089839979305700)
XLA Ops:
  0.6 41.0 %shard_map.103 = (f32[8,16,128]{2,1,0:T(8,128)S(1)}, f32[1,8,16,256]{3,2,1,0:T(8,128)S(1)}, f32[1,8,16,256]{3,2,1,0:T(8,128)S(1)}) custom-call(f32[1,8,16,256]{3,2,1,0:T(8,128)} %now.1, f32[1,8,16,256]{3,2,1,0:T(8,128)} %later.1, f32[8,16,256]{2,1,0:T(8,128)} %courant.1, f32[8,8,128]{2,1,0:T(8,128)} %strips.1, f32[8,1,1,128]{3,2,1,0:T(1,128)} %traces.1, ...), custom_call_target="tpu_custom_call" | custom-call | tf_op jit(solution)/shard_map/pallas_call | solution.py:466
  41.7 0.7 %shard_map.104 = (f32[8,16,128]{2,1,0:T(8,128)}, f32[1,8,16,256]{3,2,1,0:T(8,128)}, f32[1,8,16,256]{3,2,1,0:T(8,128)}) custom-call(f32[8,16,128]{2,1,0:T(8,128)S(1)} %get-tuple-element.6.image_in, f32[1,8,16,256]{3,2,1,0:T(8,128)S(1)} %get-tuple-element.7.now_in, f32[1,8,16,256]{3,2,1,0:T(8,128)S(1)} %get-tuple-element.8.later_in), custom_call_target="tpu_custom_call" | custom-call | tf_op jit(solution)/shard_map/pallas_call | solution.py:515

commit v5 on v4

--- a/solution.py
+++ b/solution.py
@@ -41,7 +41,7 @@
     yl, yh, cl, ch, hx, hy, inj, dense, image_in, image,
     strip_v, trace_v, cell_v, source, wavelet,
     load_sem, xs_sem, xts_sem, ys_sem, yts_sem, cs_sem, xcs_sem, ycs_sem,
-    xr_sem, xtr_sem, yr_sem, ytr_sem, cr_sem, xcr_sem, ycr_sem, im_send, im_recv, ready,
+    xr_sem, xtr_sem, yr_sem, ytr_sem, cr_sem, xcr_sem, ycr_sem, im_send, im_recv, xps_sem, xpr_sem, ready,
 ):
     group = lax.axis_index("grp")
     at_x = lax.axis_index("gx")
@@ -107,17 +107,17 @@
         return remote(ys.at[j, :, pl.ds(4 * i, 4)], cr.at[par, 1 - i, 1 - j],
                       cs_sem.at[i, j], cr_sem.at[par, 1 - i, 1 - j], {"gx": x_of[i], "gy": y_of[j]})
 
-    def xc_copy(d):
-        return remote(c.at[:, pl.ds(4 * d, 4)], xc.at[1 - d],
-                      xcs_sem.at[d], xcr_sem.at[1 - d], {"gx": x_of[d]})
-
     def x_first(d, h):
         return remote(now.at[0, pl.ds(4 * d, 4), :, pl.ds(128 * h, 128)], xr.at[0, 1 - d, h],
                       xs_sem.at[d], xr_sem.at[0, 1 - d], {"gx": x_of[d]})
 
-    def xc_first(d, h):
-        return remote(courant.at[pl.ds(4 * d, 4), :, pl.ds(128 * h, 128)], xc.at[1 - d, h],
+    def xc_first(d):
+        mine = pl.ds(pl.multiple_of(128 * group, 128), 128)
+        return remote(courant.at[pl.ds(4 * d, 4), :, mine], xc.at[1 - d, group],
                       xcs_sem.at[d], xcr_sem.at[1 - d], {"gx": x_of[d]})
+
+    def xc_pass(d):
+        return remote(xc.at[d, group], xc.at[d, group], xps_sem.at[d], xpr_sem.at[d], partner)
 
     def yc_copy(d):
         return remote(ycs.at[d], yc.at[1 - d], ycs_sem.at[d], ycr_sem.at[1 - d], {"gy": y_of[d]})
@@ -142,6 +142,8 @@
             copy.wait_send()
 
     pl.semaphore_wait(barrier, count)
+    for d in range(2):
+        start(has_x[d], xc_first(d))
     for d in range(2):
         for h in range(2):
             start(has_x[d], x_first(d, h))
@@ -151,9 +153,6 @@
         def _():
             pl.semaphore_signal(ready.at[1 - d], inc=1, device_id={"gy": y_of[d]}, device_id_type=MESH)
 
-    for d in range(2):
-        for h in range(2):
-            start(has_x[d], xc_first(d, h))
 
     for slot in range(2):
         u[slot, :, :, 0:8] = jnp.zeros((2, 8, 8, 128), F32)
@@ -365,6 +364,14 @@
             def _():
                 inject(0, step + 2)
 
+        if par == 0:
+
+            @pl.when(first)
+            def _():
+                for d in range(2):
+                    wait_recv(has_x[d], xc_first(1 - d))
+                    start(has_x[d], xc_pass(d))
+
         for d in range(2):
             wait_recv(has_y[d], y_copy(par, 1 - d))
         for x in range(8):
@@ -383,13 +390,14 @@
             @pl.when(first)
             def _():
                 for d in range(2):
-                    wait_recv(has_x[d], xc_copy(1 - d))
+                    wait_recv(has_x[d], xc_pass(d))
                     wait_recv(has_y[d], yc_copy(1 - d))
                     for h in range(2):
                         xcm[d, h] = jnp.where(overwrite[h], 0.0, xc[d, h])
                         ycm[d, h] = jnp.where(overwrite4[h], 0.0, yc[d, h])
                 for d in range(2):
-                    wait_send(has_x[d], xc_copy(d))
+                    wait_send(has_x[d], xc_first(d))
+                    wait_send(has_x[d], xc_pass(d))
                     wait_send(has_y[d], yc_copy(d))
 
         else:
@@ -507,7 +515,7 @@
             dma((11,)),
             dma((2,)), dma((2,)), dma((2,)), dma((2,)), dma((2, 2)), dma((2,)), dma((2,)),
             dma((2, 2)), dma((2, 2)), dma((2, 2)), dma((2, 2)), dma((2, 2, 2)), dma((2,)), dma((2,)),
-            dma((2,)), dma((2,)),
+            dma((2,)), dma((2,)), dma((2,)), dma((2,)),
             pltpu.SemaphoreType.REGULAR((2,)),
         ],
         compiler_params=pltpu.CompilerParams(collective_id=0, has_side_effects=True),

time: 42.6 us -> 41.9 us (0.984)
  Pallas kernels: 41.8 us -> 41.1 us
    pallas_call x1, Pallas kernels: 41 us -> 40.4 us  [local(): pl.pallas_call(kernel, out_shape=(v((8, 16, 128), F32), v((1, 8, 16, 256)...]
where the time goes in v5:
time: 41.9 us; the launch traced here: 41.7 us
  Pallas kernels  41.1 us (98%)
  between operations  0.64 us (2%)
    pallas_call x1, Pallas kernels, local(): pl.pallas_call(kernel, out_shape=(v((8, 16, 128), F32), v((1, 8, 16, 256)...  40.4 us

profile of v5, /device:TPU:7, one launch (start us, length us, event | category | flops | bytes accessed | tf_op | source)
XLA Modules:
  0.0 41.7 jit_solution(8372172873418336598)
XLA Ops:
  0.6 40.4 %shard_map.103 = (f32[8,16,128]{2,1,0:T(8,128)S(1)}, f32[1,8,16,256]{3,2,1,0:T(8,128)S(1)}, f32[1,8,16,256]{3,2,1,0:T(8,128)S(1)}) custom-call(f32[1,8,16,256]{3,2,1,0:T(8,128)} %now.1, f32[1,8,16,256]{3,2,1,0:T(8,128)} %later.1, f32[8,16,256]{2,1,0:T(8,128)} %courant.1, f32[8,8,128]{2,1,0:T(8,128)} %strips.1, f32[8,1,1,128]{3,2,1,0:T(1,128)} %traces.1, ...), custom_call_target="tpu_custom_call" | custom-call | tf_op jit(solution)/shard_map/pallas_call | solution.py:474
  41.0 0.7 %shard_map.104 = (f32[8,16,128]{2,1,0:T(8,128)}, f32[1,8,16,256]{3,2,1,0:T(8,128)}, f32[1,8,16,256]{3,2,1,0:T(8,128)}) custom-call(f32[8,16,128]{2,1,0:T(8,128)S(1)} %get-tuple-element.6.image_in, f32[1,8,16,256]{3,2,1,0:T(8,128)S(1)} %get-tuple-element.7.now_in, f32[1,8,16,256]{3,2,1,0:T(8,128)S(1)} %get-tuple-element.8.later_in), custom_call_target="tpu_custom_call" | custom-call | tf_op jit(solution)/shard_map/pallas_call | solution.py:523

commit v6 on v5

--- a/solution.py
+++ b/solution.py
@@ -103,6 +103,10 @@
         return remote(yts.at[d], ytr.at[par, 1 - d],
                       yts_sem.at[d], ytr_sem.at[par, 1 - d], {"gy": y_of[d]})
 
+    def y_half(par, e, d):
+        return remote(ys.at[e, :, pl.ds(4 * d, 4)], yr.at[par, 1 - e, :, pl.ds(4 * d, 4)],
+                      ys_sem.at[e], yr_sem.at[par, 1 - e], {"gy": y_of[e]})
+
     def corner_copy(par, i, j):
         return remote(ys.at[j, :, pl.ds(4 * i, 4)], cr.at[par, 1 - i, 1 - j],
                       cs_sem.at[i, j], cr_sem.at[par, 1 - i, 1 - j], {"gx": x_of[i], "gy": y_of[j]})
@@ -124,6 +128,11 @@
 
     def image_copy(slot):
         return remote(u.at[0, 1 - group, :, pl.ds(8, 16)], image_in.at[slot],
+                      im_send.at[slot], im_recv.at[slot], partner)
+
+    def image_half(slot, d):
+        planes = pl.ds(4 * d, 4)
+        return remote(u.at[0, 1 - group, planes, pl.ds(8, 16)], image_in.at[slot, planes],
                       im_send.at[slot], im_recv.at[slot], partner)
 
     def start(there, copy):
@@ -427,8 +436,10 @@
             for j in range(2):
                 start(jnp.logical_and(more, has_c[d, j]), corner_copy(1 - par, d, j))
             start(jnp.logical_and(more, has_x[d]), x_copy(1 - par, d))
-        for d in range(2):
-            start(jnp.logical_and(more, has_y[d]), y_copy(1 - par, d))
+            for e in range(2):
+                start(jnp.logical_and(more, has_y[e]), y_half(1 - par, e, d))
+            if par == 1:
+                start(final, image_half(1, d))
         for d in range(2):
             wait_send(has_x[d], xt_copy(par, d))
             wait_send(has_y[d], yt_copy(par, d))
@@ -440,10 +451,6 @@
             def _():
                 image_copy(0).start()
                 send_t(1 - par)
-
-            @pl.when(final)
-            def _():
-                image_copy(1).start()
 
     def two_rounds(half, carry):
         one_round(half, 0)

time: 41.9 us -> 41.9 us (level)
  no operation moved by 1% of the time
where the time goes in v6:
time: 41.9 us; the launch traced here: 41.7 us
  Pallas kernels  41.1 us (98%)
  between operations  0.64 us (2%)
    pallas_call x1, Pallas kernels, local(): pl.pallas_call(kernel, out_shape=(v((8, 16, 128), F32), v((1, 8, 16, 256)...  40.3 us

profile of v6, /device:TPU:7, one launch (start us, length us, event | category | flops | bytes accessed | tf_op | source)
XLA Modules:
  0.0 41.7 jit_solution(7177514904009392617)
XLA Ops:
  0.6 40.3 %shard_map.103 = (f32[8,16,128]{2,1,0:T(8,128)S(1)}, f32[1,8,16,256]{3,2,1,0:T(8,128)S(1)}, f32[1,8,16,256]{3,2,1,0:T(8,128)S(1)}) custom-call(f32[1,8,16,256]{3,2,1,0:T(8,128)} %now.1, f32[1,8,16,256]{3,2,1,0:T(8,128)} %later.1, f32[8,16,256]{2,1,0:T(8,128)} %courant.1, f32[8,8,128]{2,1,0:T(8,128)} %strips.1, f32[8,1,1,128]{3,2,1,0:T(1,128)} %traces.1, ...), custom_call_target="tpu_custom_call" | custom-call | tf_op jit(solution)/shard_map/pallas_call | solution.py:481
  41.0 0.7 %shard_map.104 = (f32[8,16,128]{2,1,0:T(8,128)}, f32[1,8,16,256]{3,2,1,0:T(8,128)}, f32[1,8,16,256]{3,2,1,0:T(8,128)}) custom-call(f32[8,16,128]{2,1,0:T(8,128)S(1)} %get-tuple-element.6.image_in, f32[1,8,16,256]{3,2,1,0:T(8,128)S(1)} %get-tuple-element.7.now_in, f32[1,8,16,256]{3,2,1,0:T(8,128)S(1)} %get-tuple-element.8.later_in), custom_call_target="tpu_custom_call" | custom-call | tf_op jit(solution)/shard_map/pallas_call | solution.py:530
